TPU v7x, 128 devices: a whole 4x4x4 slice. The times are simulated.
128 devices in a mesh: seq: 4 (over z), tp: 32 (over y, x, core).
Axes of the slice: x: 4, y: 4, z: 4, core: 2. Of those that a mesh axis runs over, the one named last changes fastest.
Arguments:
- residual: bfloat16 [8192, 2048], P('seq', 'tp'), may hold values from -6 to 6
- attn_gain: bfloat16 [2048], replicated, may hold values from 0.25 to 1.75
- attn_in: bfloat16 [3, 2048, 2048], P(None, None, 'tp')
- attn_out: bfloat16 [2048, 2048], P('tp'), may hold values from -0.125 to 0.125
- ffn_gain: bfloat16 [2048], replicated, may hold values from 0.25 to 1.75
- ffn_in: bfloat16 [2, 2048, 20480], P(None, None, 'tp'), may hold values from -0.125 to 0.125
- ffn_out: bfloat16 [20480, 2048], P('tp'), may hold values from -0.0390625 to 0.0390625
- route_rows: int32 [4, 224], P('seq'), may hold values from 0 to 2047, as said below
- route_counts: int32 [4], replicated, may hold values from 1 to 224, 512 in all
Outputs:
- layer_out: bfloat16 [8192, 2048], P('seq', 'tp')
Inputs may be any that keep to these rules, and one draw needn't show every extreme that they name: `route_rows`: in each row s the 224 entries are distinct positions of that shard; only the first route_counts[s] entries are used; each row holds 0 and 2047. `route_counts`: the counts sum to 512 and the largest is exactly 224.
All inputs are finite; a program needn't handle non-finite values.
Results may differ from a plain program's by a relative error of at most 0.014.
Values may be sent and summed in bfloat16 or wider, within the bound.
A program may use at most 64 MiB of HBM per device.

v0:
```python
import jax
import jax.numpy as jnp
from jax import lax
from jax.sharding import PartitionSpec as P

HD = 64
RADIUS = 127


epsilon = 1e-06


def extended(block, sides, width):
    for axis, dim in sides:
        count = lax.axis_size(axis)
        forward = [(i, i + 1) for i in range(count - 1)]
        backward = [(target, source) for source, target in forward]
        low = lax.ppermute(
            lax.slice_in_dim(block, block.shape[dim] - width, None, axis=dim), axis, forward
        )
        high = lax.ppermute(lax.slice_in_dim(block, 0, width, axis=dim), axis, backward)
        block = jnp.concatenate([low, block, high], axis=dim)
    return block


def rms_norm(values, gain_row):
    wide = values.astype(jnp.float32)
    mean_square = jnp.mean(wide * wide, axis=-1, keepdims=True)
    return (wide * lax.rsqrt(mean_square + epsilon) * gain_row.astype(jnp.float32)).astype(
        jnp.bfloat16
    )


def heavy_branch(rows_part, ffn_gain, ffn_in, ffn_out):
    full_rows = lax.all_gather(rows_part, "tp", axis=1, tiled=True)
    normed_rows = rms_norm(full_rows, ffn_gain)
    both = jnp.einsum("nd,kdf->knf", normed_rows, ffn_in, preferred_element_type=jnp.float32)
    hidden = (jax.nn.gelu(both[0], approximate=True) * both[1]).astype(jnp.bfloat16)
    partial_value = jnp.dot(hidden, ffn_out, preferred_element_type=jnp.float32)
    return lax.psum_scatter(
        partial_value.astype(jnp.bfloat16), "tp", scatter_dimension=1, tiled=True
    ).astype(jnp.float32)


def local(
    residual, attn_gain, attn_in, attn_out, ffn_gain, ffn_in, ffn_out, route_rows, route_counts
):
    seq_count = lax.axis_size("seq")
    seq_index = lax.axis_index("seq")
    whole = lax.all_gather(residual, "tp", axis=1, tiled=True)
    tok_rows = whole.shape[0]
    normed = rms_norm(whole, attn_gain)
    projected = jnp.einsum(
        "td,kdh->kth", normed, attn_in, preferred_element_type=jnp.float32
    ).astype(jnp.bfloat16)
    local_width = projected.shape[2]
    local_heads = local_width // HD
    paired = jnp.concatenate([projected[1], projected[2]], axis=1)
    padded = extended(paired, (("seq", 0),), RADIUS)
    block = min(512, tok_rows)
    span = block + 2 * RADIUS
    queries_all = projected[0]

    def attend(block_id):
        start = block_id * block
        query_blk = lax.dynamic_slice_in_dim(queries_all, start, block, 0).reshape(
            block, local_heads, HD
        )
        both_blk = lax.dynamic_slice_in_dim(padded, start, span, 0)
        key_blk = both_blk[:, :local_width].reshape(span, local_heads, HD)
        value_blk = both_blk[:, local_width:].reshape(span, local_heads, HD)
        query_pos = seq_index * tok_rows + start + jnp.arange(block, dtype=jnp.int32)
        key_pos = seq_index * tok_rows + start - RADIUS + jnp.arange(span, dtype=jnp.int32)
        usable = (
            (jnp.abs(query_pos[:, None] - key_pos[None, :]) <= RADIUS)
            & (key_pos[None, :] >= 0)
            & (key_pos[None, :] < seq_count * tok_rows)
        )
        scores = (
            jnp.einsum("qhd,khd->hqk", query_blk, key_blk, preferred_element_type=jnp.float32)
            / HD**0.5
        )
        scores = jnp.where(usable[None], scores, -jnp.inf)
        top = jnp.max(scores, axis=-1, keepdims=True)
        expo = jnp.exp(scores - top)
        prob_rows = (expo / jnp.sum(expo, axis=-1, keepdims=True)).astype(jnp.bfloat16)
        context_blk = jnp.einsum(
            "hqk,khd->qhd", prob_rows, value_blk, preferred_element_type=jnp.float32
        )
        return context_blk.astype(jnp.bfloat16).reshape(block, local_width)

    context = lax.map(attend, jnp.arange(tok_rows // block, dtype=jnp.int32)).reshape(
        tok_rows, local_width
    )
    partial_mix = jnp.dot(context, attn_out, preferred_element_type=jnp.float32)
    mixed = lax.psum_scatter(
        partial_mix.astype(jnp.bfloat16), "tp", scatter_dimension=1, tiled=True
    ).astype(jnp.float32)
    updated = (residual.astype(jnp.float32) + mixed).astype(jnp.bfloat16)
    slot_total = route_rows.shape[1]
    slots = jnp.arange(slot_total, dtype=jnp.int32)
    row_index = route_rows[0]
    row_count = lax.dynamic_index_in_dim(route_counts, seq_index, 0, keepdims=False)
    usable_slots = slots < row_count
    taken = jnp.take(updated, row_index, axis=0)
    heavy = heavy_branch(taken, ffn_gain, ffn_in, ffn_out)
    heavy = jnp.where(usable_slots[:, None], heavy, 0.0)
    result = updated.astype(jnp.float32).at[row_index].add(heavy)
    return result.astype(jnp.bfloat16)


def solution(mesh):
    in_specs = (
        P("seq", "tp"),
        P(),
        P(None, None, "tp"),
        P("tp", None),
        P(),
        P(None, None, "tp"),
        P("tp", None),
        P("seq", None),
        P(),
    )
    out_specs = P("seq", "tp")
    return jax.shard_map(local, mesh=mesh, in_specs=in_specs, out_specs=out_specs, check_vma=False)
```

profile of v0, /device:TPU:1, one launch (start us, length us, event | category | flops | bytes accessed | tf_op | source)
XLA Modules:
  0.0 332.9 jit_solution(8684373706657008721)
XLA Ops:
  6.5 0.0 copy-start
  6.5 0.0 all-gather.2.cloned.1.call-start
  6.5 0.7 all-gather.2.cloned.1.call-update
  7.3 0.0 reduce-scatter.3.cloned.1.call-start
  7.3 0.7 convert_element_type.72
  8.0 57.8 %all-gather.2.cloned.1.call-done = bf16[2048,2048]{0,1:T(8,128)(2,1)} async-done(((bf16[2048,64]{0,1:T(8,128)(2,1)}), bf16[2048,2048]{0,1:T(8,128)(2,1)}) %all-gather.2.cloned.1.call-update) | async-done | bytes 8388624 | tf_op jit(solution)/shard_map/all_gather | solution.py:50
  65.9 5.3 %fusion.11 = f32[2048]{0:T(1024)S(1)} fusion(bf16[2048,2048]{0,1:T(8,128)(2,1)} %all-gather.2.cloned.1.call-done), kind=kLoop, calls=%fused_computation.22 | loop fusion | flops 12580864 | bytes 8396800 | tf_op jit(solution)/shard_map/reduce_sum | solution.py:28
  71.2 0.5 copy-done.2
  71.6 3.5 %fusion.14 = f32[2048,192]{0,1:S(1)} fusion(bf16[2048,192]{0,1:T(8,128)(2,1)} %bitcast.58, bf16[2048,2048]{0,1:T(8,128)(2,1)S(1)} %copy-done.2, f32[2048]{0:T(1024)S(1)} %convert_element_type.72, f32[2048]{0:T(1024)S(1)} %add_rsqrt_fusion), kind=kOutput, calls=%fused_computation.25 | convolution fusion | flops 1627389952 | bytes 10764288
  75.2 0.1 convert_bitcast_fusion
  75.3 0.8 slice_bitcast_fusion.2
  76.0 0.1 fusion.40
  76.1 3.2 collective-permute-start
  79.3 1.3 collective-permute-start.1
  80.7 0.0 collective-permute-done
  80.7 3.3 collective-permute-done.1
  84.0 1.3 concatenate.7
  85.3 27.3 %while.12 = (s32[]{:T(128)}, bf16[4,512,64]{1,2,0:T(8,128)(2,1)S(1)}, s32[4]{0:T(128)S(1)}, bf16[2302,128]{0,1:T(8,128)(2,1)}, s32[]{:T(128)}, /*index=5*/bf16[2...) while((s32[]{:T(128)}, ...), condition=%wide.region_4.5_spmd, body=%wide.region_1.4_spmd.sunk | while | flops 105534976 | bytes 11337492 | solution.py:92
  85.3 0.6 dynamic_slice.31
  86.6 1.8 fusion.58
  88.4 1.2 copy-done.1
  89.6 0.4 fusion.59
  90.0 2.1 fusion.60
  92.1 0.6 dynamic_slice.31
  93.4 1.8 fusion.58
  95.3 1.2 copy-done.1
  96.4 0.4 fusion.59
  96.8 2.1 fusion.60
  99.0 0.6 dynamic_slice.31
  100.2 1.9 fusion.58
  102.1 1.2 copy-done.1
  103.3 0.4 fusion.59
  103.7 2.1 fusion.60
  105.8 0.6 dynamic_slice.31
  107.1 1.8 fusion.58
  108.9 1.2 copy-done.1
  110.1 0.4 fusion.59
  110.5 2.1 fusion.60
  112.6 0.0 copy-done.4
  112.6 5.6 %convolution_convert_fusion.1 = bf16[2048,2048]{0,1:T(8,128)(2,1)} fusion(bf16[2048,64]{0,1:T(8,128)(2,1)S(1)} %bitcast.53, bf16[64,2048]{1,0:T(8,128)(2,1)S(1)} %copy-done.4), kind=kOutput, calls=%fused_computation.28 | convolution fusion | flops 541065216 | bytes 8912896 | tf_op jit(solution)/shard_map/dot_general | solution.py:95
  118.2 0.0 reduce-scatter.3.cloned.1.call-update
  118.3 0.0 reduce-scatter.5.cloned.1.call-start
  118.3 0.6 copy-done.5
  118.9 0.0 copy-done.6
  119.0 90.7 %reduce-scatter.3.cloned.1.call-done = bf16[2048,64]{0,1:T(8,128)(2,1)} async-done(((bf16[2048,2048]{0,1:T(8,128)(2,1)}), bf16[2048,64]{0,1:T(8,128)(2,1)}) %reduce-scatter.3.cloned.1.call-update) | async-done | bytes 262160 | tf_op jit(solution)/shard_map/reduce_scatter | solution.py:96
  209.6 1.0 add_convert_fusion
  210.7 0.3 copy.36
  210.9 0.8 gather_fusion
  211.8 0.1 broadcast_select_fusion
  211.9 0.1 copy.37
  212.0 26.7 %all_gather.7 = bf16[224,2048]{0,1:T(8,128)(2,1)S(1)} all-gather(bf16[224,64]{0,1:T(8,128)(2,1)S(1)} %copy.37), channel_id=1, replica_groups=mesh['seq'=4,'tp'=32] {'tp'}, dimensions={1}, use_global_device_ids=true | all-gather | bytes 946176 | tf_op jit(solution)/shard_map/all_gather | solution.py:35
  238.7 0.3 fusion.18
  239.0 4.0 %convolution_bitcast_fusion = f32[2,224,640]{2,1,0:T(8,128)S(1)} fusion(bf16[2,2048,640]{2,1,0:T(8,128)(2,1)} %param.16, bf16[224,2048]{0,1:T(8,128)(2,1)S(1)} %all_gather.7, f32[2048]{0:T(1024)S(1)} %convert_element_type.81, f32[224]{0:T(256)S(1)} %add_rsqrt_fusion.1), kind=kOutput, calls=%fused_computation.35 | convolution fusion | flops 1176240128 | bytes 7316352 | tf_op jit(solution)/shard_map/nd,kdf->knf/dot_general | solution.py:37
  243.1 0.0 copy-start.7
  243.1 2.3 convolution_convert_fusion.2
  245.4 0.0 reduce-scatter.5.cloned.1.call-update
  245.4 0.6 dynamic_slice.23
  246.0 0.6 iota_compare_fusion
  246.7 1.2 copy.39
  247.8 71.7 %reduce-scatter.5.cloned.1.call-done = bf16[224,64]{0,1:T(8,128)(2,1)} async-done(((bf16[224,2048]{0,1:T(8,128)(2,1)}), bf16[224,64]{0,1:T(8,128)(2,1)}) %reduce-scatter.5.cloned.1.call-update) | async-done | bytes 28688 | tf_op jit(solution)/shard_map/reduce_scatter | solution.py:40
  319.6 0.8 convert_select_fusion
  320.3 0.1 copy.40
  320.4 3.8 %scatter_fusion = f32[2048,64]{1,0:T(8,128)} fusion(f32[2048,64]{1,0:T(8,128)} %copy.39, s32[224]{0:T(256)S(1)} %bitcast.56, f32[224,64]{1,0:T(8,128)S(1)} %copy.40), kind=kCustom, calls=%fused_computation.1 | custom fusion | flops 14336 | bytes 172928 | tf_op jit(solution)/shard_map/scatter-add | solution.py:108
  324.2 2.1 copy.41
  (34 shorter events, 0.2 us)
Async XLA Ops:
  6.5 236.5 %copy-start = (bf16[640,2048]{1,0:T(8,128)(2,1)S(1)}, bf16[640,2048]{1,0:T(8,128)(2,1)}, u32[]{:S(2)}) copy-start(bf16[640,2048]{1,0:T(8,128)(2,1)} %param.17) | copy-start | bytes 7864324
  6.5 59.3 %all-gather.2.cloned.1.call-start = ((), (), s32[]{:S(2)}) async-start(), calls=%async_computation.2 | async-start | bytes 8650752 | tf_op jit(solution)/shard_map/all_gather | solution.py:50
  7.3 202.4 %reduce-scatter.3.cloned.1.call-start = ((), (), s32[]{:S(2)}) async-start(), calls=%async_computation.3 | async-start | bytes 8650752 | tf_op jit(solution)/shard_map/reduce_scatter | solution.py:96
  65.9 5.8 %copy-start.2 = (bf16[2048,2048]{0,1:T(8,128)(2,1)S(1)}, bf16[2048,2048]{0,1:T(8,128)(2,1)}, u32[]{:S(2)}) copy-start(bf16[2048,2048]{0,1:T(8,128)(2,1)} %all-gather.2.cloned.1.call-done) | copy-start | bytes 25165828
  76.1 4.5 %collective-permute-start = (bf16[127,128]{0,1:T(8,128)(2,1)S(1)}, bf16[127,128]{0,1:T(8,128)(2,1)S(1)}, u32[]{:S(2)}, u32[]{:S(2)}) collective-permute-start(bf16[127,128]{0,1:T(8,128)(2,1)S(1)} %get-tuple-element.129), channel_id=1, source_target_pairs={{0,32},{32,64},{64,96},{1,33},{33,65},{65,97},{2,34},{34,66},{66,9... | collective-permute-start | bytes 97544 | tf_op jit(solution)/shard_map/ppermute | solution.py:18
  79.3 4.7 %collective-permute-start.1 = (bf16[127,128]{0,1:T(8,128)(2,1)S(1)}, bf16[127,128]{0,1:T(8,128)(2,1)S(1)}, u32[]{:S(2)}, u32[]{:S(2)}) collective-permute-start(bf16[127,128]{0,1:T(8,128)(2,1)S(1)} %get-tuple-element.128), channel_id=1, source_target_pairs={{32,0},{64,32},{96,64},{33,1},{65,33},{97,65},{34,2},{66,34},{98,6... | collective-permute-start | bytes 97544 | tf_op jit(solution)/shard_map/ppermute | solution.py:21
  85.3 27.3 %copy-start.4 = (bf16[64,2048]{1,0:T(8,128)(2,1)S(1)}, bf16[64,2048]{1,0:T(8,128)(2,1)}, u32[]{:S(2)}) copy-start(bf16[64,2048]{1,0:T(8,128)(2,1)} %param.14) | copy-start | bytes 786436
  88.4 1.2 copy-start.1
  95.3 1.2 copy-start.1
  102.1 1.2 copy-start.1
  108.9 1.2 copy-start.1
  118.2 0.7 copy-start.5
  118.2 0.7 copy-start.6
  118.2 91.4 %copy-start.3 = (bf16[2048,64]{0,1:T(8,128)(2,1)S(1)}, bf16[2048,64]{0,1:T(8,128)(2,1)}, u32[]{:S(2)}) copy-start(bf16[2048,64]{0,1:T(8,128)(2,1)} %param.11) | copy-start | bytes 786436
  118.3 201.3 %reduce-scatter.5.cloned.1.call-start = ((), (), s32[]{:S(2)}) async-start(), calls=%async_computation.4 | async-start | bytes 1081344 | tf_op jit(solution)/shard_map/reduce_scatter | solution.py:40
  243.1 2.4 copy-start.7
Sparse Core Ops, SparseCore 0:
  9.6 56.2 all-gather.1
  118.4 91.2 reduce-scatter.2
  245.5 74.0 reduce-scatter.4
where the time goes:
time: 335 us; the launch traced here: 333 us
  waiting for transfers between devices  224 us (67%)
  matrix products  31.4 us (9%)
  blocking collectives  26.7 us (8%)
  local copies, waits for them, and re-layouts  15.5 us (5%)
  other arithmetic  14.5 us (4%)
  between operations  13.3 us (4%)
  starting transfers between devices  4.56 us (1%)
    reduce_scatter x1, waiting for transfers between devices, local(): lax.psum_scatter(partial_mix.astype(jnp.bfloat16), 'tp', scatter_dimensio...  90.7 us
    reduce_scatter x1, waiting for transfers between devices, heavy_branch(): lax.psum_scatter(partial_value.astype(jnp.bfloat16), 'tp', scatter_dimens...  71.7 us
    all_gather x1, waiting for transfers between devices, local(): whole = lax.all_gather(residual, 'tp', axis=1, tiled=True)  57.8 us
    all_gather x1, blocking collectives, heavy_branch(): full_rows = lax.all_gather(rows_part, 'tp', axis=1, tiled=True)  26.7 us
    dot_general x4, matrix products, attend(): jnp.einsum('hqk,khd->qhd', prob_rows, value_blk, preferred_element_type=j...  8.49 us
    dot_general x4, matrix products, attend(): jnp.einsum('qhd,khd->hqk', query_blk, key_blk, preferred_element_type=jnp...  7.39 us
  transfers between devices with their start and end apart: 5, of which 4 were waited for; matrix products, arithmetic and copies ran while one was open for 1% of the time, Pallas kernels for 0%

commit v1 on v0

v1 whole, which is shorter than its diff:
```python
import jax
import jax.numpy as jnp
from jax import lax
from jax.experimental import pallas as pl
from jax.experimental.pallas import tpu as pltpu
from jax.sharding import PartitionSpec as P

MESH = pl.DeviceIdType.MESH
F32 = jnp.float32
BF16 = jnp.bfloat16
EPS = 1e-06
RADIUS = 127
NEG = -1e30
SIDE = 4
CHIPS = SIDE * SIDE
TOK = 2048
HALF = TOK // 2
BAND = HALF // 2
QUART = BAND // 2
LANES = 128
FEAT = CHIPS * LANES
HEADW = 64
CAP = 224
CAPC = CAP // 2
FFU = 640
HALO = 128
QBLK = 128


def gelu(v):
    return 0.5 * v * (1.0 + jnp.tanh(0.7978845608028654 * (v + 0.044715 * v * v * v)))


def kernel(
    res, wqkv, wout, ffi, ffo, gains, route, counts,
    out,
    xa, xo, wa, wb, wo, fi, fo, w2, xg, acc, ssq, qs, kv, ctx, bias, oh, oht,
    pb, rx1, rx2, upd, gp, pk, px, nrm, hid, pb2, rxc, sb, rxh, hv, om, ot,
    lsem, psend, precv, gsend, grecv, hsend, hrecv, r1send, r1recv, r2send, r2recv,
    asend, arecv, fsend, frecv, hvsend, hvrecv,
):
    z = lax.axis_index("seq")
    tp = lax.axis_index("tp")
    core = lax.rem(tp, 2)
    chip = tp // 2
    x = lax.rem(chip, SIDE)
    y = chip // SIDE
    partner = tp + 1 - 2 * core

    def wrap(v):
        return lax.rem(v + 2 * SIDE, SIDE)

    def chip_at(cx, cy):
        return wrap(cy) * SIDE + wrap(cx)

    def tp_at(cx, cy):
        return chip_at(cx, cy) * 2 + core

    def remote(src, dst, ssem, rsem, dev):
        return pltpu.make_async_remote_copy(
            src_ref=src, dst_ref=dst, send_sem=ssem, recv_sem=rsem, device_id=dev, device_id_type=MESH
        )

    def block(h, da, db):
        return chip_at(x + da, y + db) if h == 0 else chip_at(x + db, y + da)

    def near(h, axis, step):
        if (axis == 0) == (h == 0):
            return {"tp": tp_at(x + step, y)}
        return {"tp": tp_at(x, y + step)}

    SIGN = (1, -1)
    mine = pl.multiple_of(core * HALF, HALF)
    theirs = pl.multiple_of((1 - core) * HALF, HALF)

    loads = [
        pltpu.make_async_copy(res.at[pl.ds(mine, HALF)], xa, lsem.at[0]),
        pltpu.make_async_copy(wqkv, wa, lsem.at[1]),
        pltpu.make_async_copy(wout, wo.at[pl.ds(pl.multiple_of(core * HEADW, HEADW), HEADW)], lsem.at[2]),
        pltpu.make_async_copy(ffi, fi, lsem.at[3]),
        pltpu.make_async_copy(ffo, fo, lsem.at[4]),
    ]
    loads[0].start()
    loads[1].start()
    loads[2].start()

    prev_dev = {"seq": lax.rem(z + 3 + core, 4), "tp": partner}
    next_dev = {"seq": lax.rem(z + core, 4), "tp": partner}
    z_peer = {"seq": lax.rem(z + 3 + 2 * core, 4), "tp": partner}
    barrier = pltpu.get_barrier_semaphore()
    peers = [near(0, 0, 1), near(0, 0, -1), near(0, 1, 1), near(0, 1, -1), {"tp": partner}, z_peer]
    for dev in peers:
        pl.semaphore_signal(barrier, inc=1, device_id=dev, device_id_type=MESH)
    pl.semaphore_wait(barrier, len(peers))

    p_x = remote(res.at[pl.ds(theirs, HALF)], xo, psend.at[0], precv.at[0], {"tp": partner})
    p_w = remote(wqkv, wb, psend.at[1], precv.at[1], {"tp": partner})
    p_o = remote(
        wout, wo.at[pl.ds(pl.multiple_of(core * HEADW, HEADW), HEADW)], psend.at[2], precv.at[2], {"tp": partner}
    )
    p_x.start()
    p_w.start()
    p_o.start()
    loads[0].wait()
    p_x.wait_recv()
    first = core == 0
    xg[chip] = jnp.where(
        first,
        jnp.concatenate([xa[...], xo[...]], axis=1),
        jnp.concatenate([xo[...], xa[...]], axis=1),
    )

    def rows(h, part):
        base = h * BAND
        if part is None:
            return pl.ds(base, BAND)
        return pl.ds(base + part * QUART, QUART)

    def g_copy(h, item, d, index, part, axis):
        src = xg.at[index, rows(h, part)]
        return remote(src, src, gsend.at[h, item, d], grecv.at[h, item, d], near(h, axis, SIGN[d]))

    def g_item(h, item, d):
        s = SIGN[d]
        table = {
            0: (block(h, 0, 0), None, 0),
            1: (block(h, 0, 0), None, 1),
            2: (block(h, -s, 0), d, 0),
            3: (block(h, -1, 0), None, 1),
            4: (block(h, 1, 0), None, 1),
            5: (block(h, 0, -s), d, 1),
            6: (block(h, 2, 0), None, 1),
            7: (block(h, -1, -s), d, 1),
            8: (block(h, 1, -s), d, 1),
            9: (block(h, 2, -s), d, 1),
        }
        index, part, axis = table[item]
        return g_copy(h, item, d, index, part, axis)

    def g_start(item):
        for h in range(2):
            for d in range(2):
                g_item(h, item, d).start()

    def g_wait(item):
        for h in range(2):
            for d in range(2):
                g_item(h, item, d).wait_recv()

    g_start(0)
    g_start(1)
    loads[3].start()
    loads[4].start()

    loads[1].wait()
    p_w.wait_recv()

    def prep_w(k, carry):
        at = pl.ds(pl.multiple_of(k * LANES, LANES), LANES)
        r_i = lax.broadcasted_iota(jnp.int32, (LANES, LANES), 0)
        c_i = lax.broadcasted_iota(jnp.int32, (LANES, LANES), 1)
        gain_col = jnp.sum(jnp.where(r_i == c_i, gains[0, k], 0.0), axis=1, keepdims=True)
        for p in range(3):
            own = wa[p, at, :]
            oth = wb[p, at, :]
            both = jnp.where(
                first, jnp.concatenate([own, oth], axis=1), jnp.concatenate([oth, own], axis=1)
            )
            w2[k, :, p * LANES : (p + 1) * LANES] = (both.astype(F32) * gain_col).astype(BF16)
        return carry

    lax.fori_loop(0, CHIPS, prep_w, 0)

    g_wait(0)
    g_start(2)
    g_start(3)
    g_start(4)

    acc[...] = jnp.zeros_like(acc)
    ssq[...] = jnp.zeros_like(ssq)

    def qkv_pair(i1, i2):
        wpair = jnp.concatenate([w2[i1], w2[i2]], axis=0)

        def step(t, carry):
            at = pl.ds(pl.multiple_of(t * QUART, QUART), QUART)
            b1 = xg[i1, at]
            b2 = xg[i2, at]
            acc[at] += jnp.dot(jnp.concatenate([b1, b2], axis=1), wpair, preferred_element_type=F32)
            f1 = b1.astype(F32)
            f2 = b2.astype(F32)
            ssq[at] += f1 * f1 + f2 * f2
            return carry

        lax.fori_loop(0, HALF // QUART, step, 0)

    def route_tables():
        row = route[...].astype(F32)
        r_i = lax.broadcasted_iota(jnp.int32, (CAP, CAP), 0)
        c_i = lax.broadcasted_iota(jnp.int32, (CAP, CAP), 1)
        shift = (core * HALF).astype(F32)
        col = jnp.sum(jnp.where(r_i == c_i, row, 0.0), axis=1, keepdims=True) - shift
        lane = lax.broadcasted_iota(jnp.int32, (CAP, HALF), 1).astype(F32)
        oh[...] = jnp.where(lane == col, 1.0, 0.0).astype(BF16)
        sub = lax.broadcasted_iota(jnp.int32, (HALF, CAP), 0).astype(F32)
        oht[...] = jnp.where(sub == row - shift, 1.0, 0.0).astype(BF16)
        q_i = lax.broadcasted_iota(jnp.int32, (QBLK, 3 * QBLK), 0)
        k_i = lax.broadcasted_iota(jnp.int32, (QBLK, 3 * QBLK), 1) - QBLK
        band = jnp.where(jnp.abs(q_i - k_i) <= RADIUS, 0.0, NEG)
        no_prev = jnp.where(z + core == 0, NEG, 0.0)
        no_next = jnp.where(z + core == 4, NEG, 0.0)
        bias[0] = band + jnp.where(k_i < 0, no_prev, 0.0)
        bias[1] = band
        bias[2] = band + jnp.where(k_i >= QBLK, no_next, 0.0)

    route_tables()

    g_wait(1)
    g_start(5)
    qkv_pair(chip_at(x - 1, y), chip_at(x + 1, y))
    g_wait(2)
    g_start(6)
    qkv_pair(chip_at(x, y - 1), chip_at(x, y + 1))
    g_wait(3)
    g_start(7)
    g_wait(4)
    g_start(8)
    g_wait(5)
    qkv_pair(chip_at(x - 1, y - 1), chip_at(x + 1, y - 1))
    qkv_pair(chip_at(x - 1, y + 1), chip_at(x + 1, y + 1))
    g_wait(6)
    g_start(9)
    qkv_pair(chip_at(x + 2, y), chip_at(x, y + 2))
    g_wait(7)
    g_wait(8)
    qkv_pair(chip_at(x + 2, y - 1), chip_at(x + 2, y + 1))
    qkv_pair(chip_at(x - 1, y + 2), chip_at(x + 1, y + 2))
    g_wait(9)
    qkv_pair(chip, chip_at(x + 2, y + 2))

    def finish_qkv(t, carry):
        at = pl.ds(pl.multiple_of(t * QUART, QUART), QUART)
        scale = lax.rsqrt(jnp.sum(ssq[at], axis=1, keepdims=True) * (1.0 / FEAT) + EPS)
        qs[at] = (acc[at, 0:LANES] * scale).astype(BF16)
        kv[pl.ds(pl.multiple_of(HALO + t * QUART, HALO), QUART), :] = (acc[at, LANES:] * scale).astype(BF16)
        return carry

    lax.fori_loop(0, HALF // QUART, finish_qkv, 0)

    h_prev = remote(kv.at[pl.ds(HALO, HALO)], kv.at[pl.ds(HALO + HALF, HALO)], hsend.at[0], hrecv.at[0], prev_dev)
    h_next = remote(kv.at[pl.ds(HALF, HALO)], kv.at[pl.ds(0, HALO)], hsend.at[1], hrecv.at[1], next_dev)
    h_prev.start()
    h_next.start()

    low_lane = lax.broadcasted_iota(jnp.int32, (QBLK, LANES), 1) < HEADW

    def attend(i, kind):
        at = pl.ds(pl.multiple_of(i * QBLK, QBLK), QBLK)
        keys = pl.ds(pl.multiple_of(i * QBLK, QBLK), 3 * QBLK)
        q = qs[at]
        zero = jnp.zeros_like(q)
        q2 = jnp.concatenate([jnp.where(low_lane, q, zero), jnp.where(low_lane, zero, q)], axis=0)
        s = lax.dot_general(q2, kv[keys, 0:LANES], (((1,), (1,)), ((), ())), preferred_element_type=F32)
        b = bias[kind]
        s = s * (1.0 / HEADW**0.5) + jnp.concatenate([b, b], axis=0)
        top = jnp.max(s, axis=1, keepdims=True)
        e = jnp.exp(s - top)
        total = jnp.sum(e, axis=1, keepdims=True)
        o = jnp.dot(e.astype(BF16), kv[keys, LANES:], preferred_element_type=F32) / total
        ctx[at] = jnp.where(low_lane, o[:QBLK], o[QBLK:]).astype(BF16)

    def attend_mid(i, carry):
        attend(i, 1)
        return carry

    lax.fori_loop(1, HALF // QBLK - 1, attend_mid, 0)
    h_prev.wait_recv()
    h_next.wait_recv()
    attend(0, 0)
    attend(HALF // QBLK - 1, 2)

    loads[2].wait()
    p_o.wait_recv()

    def wo_cols(index):
        return wo[:, pl.ds(pl.multiple_of(index * LANES, LANES), LANES)]

    def project(step):
        for h in range(2):
            lhs = ctx[h * BAND : (h + 1) * BAND]
            for pair in ((2, -1), (1, 0)):
                i1 = block(h, pair[0], step)
                i2 = block(h, pair[1], step)
                w = jnp.concatenate([wo_cols(i1), wo_cols(i2)], axis=1)
                o = jnp.dot(lhs, w, preferred_element_type=F32).astype(BF16)
                pb[i1, rows(h, None)] = o[:, :LANES]
                pb[i2, rows(h, None)] = o[:, LANES:]

    OFF = (2, -1, 1, 0)

    def r1_copy(h, j, kind, d):
        s = SIGN[d]
        db, part = ((2, d), (s, d), (s, 1 - d))[kind]
        src = pb.at[block(h, OFF[j], db), rows(h, part)]
        return remote(
            src, rx1.at[h, j, kind, d], r1send.at[h, j, kind, d], r1recv.at[h, j, kind, d], near(h, 1, s)
        )

    def r2_copy(h, kind, d):
        s = SIGN[d]
        da, part = ((2, d), (s, d), (s, 1 - d))[kind]
        src = pb.at[block(h, da, 0), rows(h, part)]
        return remote(src, rx2.at[h, kind, d], r2send.at[h, kind, d], r2recv.at[h, kind, d], near(h, 0, s))

    both_hd = [(h, d) for h in range(2) for d in range(2)]

    def r1_start(j, kind):
        for h, d in both_hd:
            r1_copy(h, j, kind, d).start()

    def r2_start(kind):
        for h, d in both_hd:
            r2_copy(h, kind, d).start()

    def relay1(j):
        for h, d in both_hd:
            r1_copy(h, j, 0, d).wait_recv()
            s = SIGN[d]
            index = block(h, OFF[j], s)
            at = rows(h, d)
            pb[index, at] = (pb[index, at].astype(F32) + rx1[h, j, 0, d].astype(F32)).astype(BF16)
            r1_copy(h, j, 1, d).start()

    def sum1(h, j, part):
        got = pb[block(h, OFF[j], 0), rows(h, part)].astype(F32)
        return got + rx1[h, j, 1, part].astype(F32) + rx1[h, j, 2, 1 - part].astype(F32)

    def total1(j):
        for h in range(2):
            for d in range(2):
                r1_copy(h, j, 1, d).wait_recv()
                r1_copy(h, j, 2, d).wait_recv()
            for part in range(2):
                pb[block(h, OFF[j], 0), rows(h, part)] = sum1(h, j, part).astype(BF16)

    project(2)
    r1_start(0, 0)
    r1_start(1, 0)
    r1_start(2, 0)
    project(1)
    project(-1)
    r1_start(0, 2)
    relay1(0)
    r1_start(1, 2)
    r1_start(2, 2)
    r1_start(3, 0)
    project(0)
    relay1(1)
    relay1(2)
    total1(0)
    r2_start(0)
    r1_start(3, 2)
    total1(1)
    total1(2)
    r2_start(2)
    relay1(3)
    for h, d in both_hd:
        r2_copy(h, 0, d).wait_recv()
        index = block(h, SIGN[d], 0)
        at = rows(h, d)
        pb[index, at] = (pb[index, at].astype(F32) + rx2[h, 0, d].astype(F32)).astype(BF16)
        r2_copy(h, 1, d).start()
    for h in range(2):
        for d in range(2):
            r1_copy(h, 3, 1, d).wait_recv()
            r1_copy(h, 3, 2, d).wait_recv()
            r2_copy(h, 1, d).wait_recv()
            r2_copy(h, 2, d).wait_recv()
        for part in range(2):
            mixed = sum1(h, 3, part) + rx2[h, 1, part].astype(F32) + rx2[h, 2, 1 - part].astype(F32)
            at = rows(h, part)
            upd[at] = (xg[chip, at].astype(F32) + mixed).astype(BF16)

    mine_r = pl.multiple_of(core * CAPC, 16)
    theirs_r = pl.multiple_of((1 - core) * CAPC, 16)
    pk[...] = jnp.dot(oh[...], upd[...], preferred_element_type=F32).astype(BF16)
    p_pick = remote(pk.at[pl.ds(theirs_r, CAPC)], px, psend.at[3], precv.at[3], {"tp": partner})
    p_pick.start()
    p_pick.wait_recv()
    gp[chip, pl.ds(mine_r, CAPC)] = (pk[pl.ds(mine_r, CAPC)].astype(F32) + px[...].astype(F32)).astype(BF16)

    def offset(k):
        return k % SIDE, k // SIDE

    def a_copy(k):
        dx, dy = offset(k)
        src = gp.at[chip, pl.ds(mine_r, CAPC)]
        return remote(src, src, asend.at[k], arecv.at[k], {"tp": tp_at(x + dx, y + dy)})

    def f_copy(k):
        dx, dy = offset(k)
        src = gp.at[chip_at(x - dx, y - dy), pl.ds(mine_r, CAPC)]
        return remote(src, src, fsend.at[k], frecv.at[k], {"tp": partner})

    order = [10, 2, 8, 6, 9, 11, 14, 5, 7, 13, 15, 1, 3, 4, 12]
    for k in order:
        a_copy(k).start()
    f_copy(0).start()
    for k in reversed(order):
        a_copy(k).wait_recv()
        f_copy(k).start()
    for k in range(CHIPS):
        f_copy(k).wait_recv()

    sq = jnp.zeros((CAP, LANES), F32)
    for k in range(CHIPS):
        v = gp[k].astype(F32)
        sq = sq + v * v
    scale = lax.rsqrt(jnp.sum(sq, axis=1, keepdims=True) * (1.0 / FEAT) + EPS)
    for k in range(CHIPS):
        nrm[:, k * LANES : (k + 1) * LANES] = (gp[k].astype(F32) * scale * gains[1, k]).astype(BF16)

    loads[3].wait()
    for n0, nw in ((0, 256), (256, 256), (512, 128)):
        rows_n = nrm[...]
        gate = jnp.dot(rows_n, fi[0, :, n0 : n0 + nw], preferred_element_type=F32)
        up = jnp.dot(rows_n, fi[1, :, n0 : n0 + nw], preferred_element_type=F32)
        hid[:, n0 : n0 + nw] = (gelu(gate) * up).astype(BF16)
    loads[4].wait()
    for n in range(CHIPS // 2):
        o = jnp.dot(hid[...], fo[:, n * 256 : (n + 1) * 256], preferred_element_type=F32).astype(BF16)
        pb2[2 * n] = o[:, :LANES]
        pb2[2 * n + 1] = o[:, LANES:]

    p_part = remote(pb2.at[:, pl.ds(theirs_r, CAPC)], rxc, psend.at[4], precv.at[4], {"tp": partner})
    p_part.start()
    p_part.wait_recv()
    for k in range(CHIPS):
        sb[k] = (pb2[k, pl.ds(mine_r, CAPC)].astype(F32) + rxc[k].astype(F32)).astype(BF16)

    def hv_copy(k):
        dx, dy = offset(k)
        return remote(
            sb.at[chip_at(x + dx, y + dy)], rxh.at[k], hvsend.at[k], hvrecv.at[k], {"tp": tp_at(x + dx, y + dy)}
        )

    for k in order:
        hv_copy(k).start()
    heavy = sb[chip].astype(F32)
    for k in reversed(order):
        hv_copy(k).wait_recv()
        heavy = heavy + rxh[k].astype(F32)
    slot = lax.broadcasted_iota(jnp.int32, (CAPC, LANES), 0) + core * CAPC
    heavy = jnp.where(slot < counts[z], heavy, 0.0)
    high = heavy.astype(BF16)
    hv[pl.ds(mine_r, CAPC), 0:LANES] = high
    hv[pl.ds(mine_r, CAPC), LANES:] = (heavy - high.astype(F32)).astype(BF16)
    hv_part = hv.at[pl.ds(mine_r, CAPC)]
    p_hv = remote(hv_part, hv_part, psend.at[5], precv.at[5], {"tp": partner})
    p_hv.start()
    p_hv.wait_recv()

    added = jnp.dot(oht[...], hv[...], preferred_element_type=F32)
    final = (upd[...].astype(F32) + added[:, :LANES] + added[:, LANES:]).astype(BF16)
    om[...] = jnp.where(first, final[:, :HEADW], final[:, HEADW:])
    ot[...] = jnp.where(first, final[:, HEADW:], final[:, :HEADW])
    out_part = out.at[pl.ds(mine, HALF)]
    p_out = remote(ot, out_part, psend.at[6], precv.at[6], {"tp": partner})
    p_out.start()
    l_out = pltpu.make_async_copy(om, out_part, lsem.at[5])
    l_out.start()

    for h, d in both_hd:
        for item in range(10):
            g_item(h, item, d).wait_send()
        for j in range(4):
            for kind in range(3):
                r1_copy(h, j, kind, d).wait_send()
        for kind in range(3):
            r2_copy(h, kind, d).wait_send()
    for copy in (p_x, p_w, p_o, h_prev, h_next, p_pick, p_part, p_hv):
        copy.wait_send()
    f_copy(0).wait_send()
    for k in order:
        a_copy(k).wait_send()
        f_copy(k).wait_send()
        hv_copy(k).wait_send()
    l_out.wait()
    p_out.wait()


def local(
    residual, attn_gain, attn_in, attn_out, ffn_gain, ffn_in, ffn_out, route_rows, route_counts
):
    gains = jnp.stack([attn_gain, ffn_gain]).astype(F32).reshape(2, CHIPS, 1, LANES)
    any_spec = pl.BlockSpec(memory_space=pl.ANY)
    vm = pltpu.VMEM
    dma = pltpu.SemaphoreType.DMA
    return pl.pallas_call(
        kernel,
        out_shape=jax.ShapeDtypeStruct((TOK, HEADW), BF16),
        in_specs=[any_spec] * 5
        + [pl.BlockSpec(memory_space=pltpu.VMEM)] * 2
        + [pl.BlockSpec(memory_space=pltpu.SMEM)],
        out_specs=any_spec,
        scratch_shapes=[
            vm((HALF, HEADW), BF16),
            vm((HALF, HEADW), BF16),
            vm((3, FEAT, HEADW), BF16),
            vm((3, FEAT, HEADW), BF16),
            vm((LANES, FEAT), BF16),
            vm((2, FEAT, FFU), BF16),
            vm((FFU, FEAT), BF16),
            vm((CHIPS, LANES, 3 * LANES), BF16),
            vm((CHIPS, HALF, LANES), BF16),
            vm((HALF, 3 * LANES), F32),
            vm((HALF, LANES), F32),
            vm((HALF, LANES), BF16),
            vm((HALF + 2 * HALO, 2 * LANES), BF16),
            vm((HALF, LANES), BF16),
            vm((3, QBLK, 3 * QBLK), F32),
            vm((CAP, HALF), BF16),
            vm((HALF, CAP), BF16),
            vm((CHIPS, HALF, LANES), BF16),
            vm((2, 4, 3, 2, QUART, LANES), BF16),
            vm((2, 3, 2, QUART, LANES), BF16),
            vm((HALF, LANES), BF16),
            vm((CHIPS, CAP, LANES), BF16),
            vm((CAP, LANES), BF16),
            vm((CAPC, LANES), BF16),
            vm((CAP, FEAT), BF16),
            vm((CAP, FFU), BF16),
            vm((CHIPS, CAP, LANES), BF16),
            vm((CHIPS, CAPC, LANES), BF16),
            vm((CHIPS, CAPC, LANES), BF16),
            vm((CHIPS, CAPC, LANES), BF16),
            vm((CAP, 2 * LANES), BF16),
            vm((HALF, HEADW), BF16),
            vm((HALF, HEADW), BF16),
            dma((6,)),
            dma((7,)),
            dma((7,)),
            dma((2, 10, 2)),
            dma((2, 10, 2)),
            dma((2,)),
            dma((2,)),
            dma((2, 4, 3, 2)),
            dma((2, 4, 3, 2)),
            dma((2, 3, 2)),
            dma((2, 3, 2)),
            dma((CHIPS,)),
            dma((CHIPS,)),
            dma((CHIPS,)),
            dma((CHIPS,)),
            dma((CHIPS,)),
            dma((CHIPS,)),
        ],
        compiler_params=pltpu.CompilerParams(
            collective_id=0, has_side_effects=True, vmem_limit_bytes=62 * 1024 * 1024
        ),
        name="layer",
    )(residual, attn_in, attn_out, ffn_in, ffn_out, gains, route_rows, route_counts)


def solution(mesh):
    in_specs = (
        P("seq", "tp"),
        P(),
        P(None, None, "tp"),
        P("tp", None),
        P(),
        P(None, None, "tp"),
        P("tp", None),
        P("seq", None),
        P(),
    )
    out_specs = P("seq", "tp")
    return jax.shard_map(local, mesh=mesh, in_specs=in_specs, out_specs=out_specs, check_vma=False)
```

time: 335 us -> 99.6 us (0.30)
  waiting for transfers between devices: 224 us -> 0 us
  Pallas kernels: 0 us -> 90.9 us
  matrix products: 31.4 us -> 0 us
  blocking collectives: 26.7 us -> 0 us
  other arithmetic: 14.5 us -> 0.63 us
  between operations: 13.3 us -> 0.01 us
  local copies, waits for them, and re-layouts: 15.5 us -> 7.75 us
  starting transfers between devices: 4.56 us -> 0 us
    reduce_scatter x2 -> x0, waiting for transfers between devices: 162 us -> none  [the longest x1 90.7 us: local(): lax.psum_scatter(partial_mix.astype(jnp.bfloat16), 'tp', scatter_dimensio...]
    pallas_call x0 -> x1, Pallas kernels: none -> 90.9 us  [local(): pl.pallas_call(kernel, out_shape=jax.ShapeDtypeStruct((TOK, HEADW), BF16)...]
    all_gather x1 -> x0, waiting for transfers between devices: 57.8 us -> none  [local(): whole = lax.all_gather(residual, 'tp', axis=1, tiled=True)]
    dot_general x11 -> x0, matrix products: 27.8 us -> none  [the longest x4 8.49 us: attend(): jnp.einsum('hqk,khd->qhd', prob_rows, value_blk, preferred_element_type=j...]
    all_gather x1 -> x0, blocking collectives: 26.7 us -> none  [heavy_branch(): full_rows = lax.all_gather(rows_part, 'tp', axis=1, tiled=True)]
    reduce_sum x6 -> x0, other arithmetic: 7.15 us -> none  [the longest x2 5.6 us: rms_norm(): mean_square = jnp.mean(wide * wide, axis=-1, keepdims=True)]
    while x8 -> x0, local copies, waits for them, and re-layouts: 4.67 us -> none
    ppermute x2 -> x0, starting transfers between devices: 4.48 us -> none  [the longest x1 3.19 us: extended(): lax.ppermute(lax.slice_in_dim(block, block.shape[dim] - width, None, axis...]
  transfers between devices with their start and end apart: 5 -> 0, of which waited for: 4 -> 0; matrix products, arithmetic and copies ran while one was open for 1% -> 0% of each run, Pallas kernels for 0% -> 0%
where the time goes in v1:
time: 99.6 us; the launch traced here: 99.3 us
  Pallas kernels  90.9 us (91%)
  local copies, waits for them, and re-layouts  7.75 us (8%)
    pallas_call x1, Pallas kernels, local(): pl.pallas_call(kernel, out_shape=jax.ShapeDtypeStruct((TOK, HEADW), BF16)...  90.9 us
    unnamed x2, local copies, waits for them, and re-layouts  4.43 us

profile of v1, /device:TPU:1, one launch (start us, length us, event | category | flops | bytes accessed | tf_op | source)
XLA Modules:
  0.0 99.3 jit_solution(10967983980822720381)
XLA Ops:
  0.0 0.7 copy.13
  0.7 0.7 copy.14
  1.4 0.6 maximum_convert_fusion.gains
  2.0 2.0 %copy.15.res = bf16[2048,64]{1,0:T(8,128)(2,1)} copy(bf16[2048,64]{0,1:T(8,128)(2,1)} %param.9) | data formatting | bytes 524288 | tf_op args[0]
  4.0 2.5 %copy.16.wqkv = bf16[3,2048,64]{2,1,0:T(8,128)(2,1)} copy(bf16[3,2048,64]{1,2,0:T(8,128)(2,1)} %param.11) | data formatting | bytes 1572864 | tf_op args[2]
  6.5 90.9 %layer.1 = bf16[2048,64]{1,0:T(8,128)(2,1)} custom-call(bf16[2048,64]{1,0:T(8,128)(2,1)} %copy.15.res, bf16[3,2048,64]{2,1,0:T(8,128)(2,1)} %copy.16.wqkv, bf16[64,2048]{1,0:T(8,128)(2,1)} %wout.1, bf16[2,2048,640]{2,1,0:T(8,128)(2,1)} %ffi.1, bf16[640,2048]{1,0:T(8,128)(2,1)} %ffo.1, f32[2,16,1,128]{3,2,1,0:T(1,128)} %maximum_convert_fusion.gains, ...), custom_call_target="tpu_custom_call" | custom-call | tf_op jit(solution)/shard_map/layer/pallas_call | solution.py:499
  97.4 1.9 %copy.17 = bf16[2048,64]{0,1:T(8,128)(2,1)} copy(bf16[2048,64]{1,0:T(8,128)(2,1)} %layer.1) | data formatting | bytes 524288 | tf_op jit(solution)/shard_map/layer/pallas_call | solution.py:499

commit v2 on v0

v2 whole, which is shorter than its diff:
```python
import jax
import jax.numpy as jnp
from jax import lax
from jax.experimental import pallas as pl
from jax.experimental.pallas import tpu as pltpu
from jax.sharding import PartitionSpec as P

MESH = pl.DeviceIdType.MESH
F32 = jnp.float32
BF16 = jnp.bfloat16
EPS = 1e-06
RADIUS = 127
NEG = -1e30
SIDE = 4
CHIPS = SIDE * SIDE
TOK = 2048
HALF = TOK // 2
QUART = HALF // 4
LANES = 128
FEAT = CHIPS * LANES
HEADW = 64
CAP = 224
CAPC = CAP // 2
FFU = 640
QBLK = 128
NBLK = HALF // QBLK
OFF = (2, -1, 1, 0)
SIGN = (1, -1)


def gelu(v):
    return 0.5 * v * (1.0 + jnp.tanh(0.7978845608028654 * (v + 0.044715 * v * v * v)))


def dot(a, b):
    return jnp.dot(a, b, preferred_element_type=F32)


def dot_nt(a, b):
    return lax.dot_general(a, b, (((1,), (1,)), ((), ())), preferred_element_type=F32)


def dot_tn(a, b):
    return lax.dot_general(a, b, (((0,), (0,)), ((), ())), preferred_element_type=F32)


def kernel(
    res, wqkv, wout, ffi, ffo, gain_a, gain_f, route, counts,
    out,
    wraw, wo, wot, fi, fo, w2, xg, acc, ssq, qt, kvb, ctx, bias, oh,
    pb, rx1, rx2, upd, fin, gp, pk, px, nrm, hid, pb2, rxc, sb, rxa, sb2, rxb, hv,
    lsem, xlsem, xsend, xrecv, psend, precv, gsend, grecv, hsend, hrecv,
    r1send, r1recv, r2send, r2recv, s1send, s1recv, s2send, s2recv,
    asend, arecv, fsend, frecv, csend, crecv,
):
    z = lax.axis_index("seq")
    tp = lax.axis_index("tp")
    core = lax.rem(tp, 2)
    chip = tp // 2
    x = lax.rem(chip, SIDE)
    y = chip // SIDE
    partner = {"tp": tp + 1 - 2 * core}

    def wrap(v):
        return lax.rem(v + 2 * SIDE, SIDE)

    def chip_at(cx, cy):
        return wrap(cy) * SIDE + wrap(cx)

    def tp_at(cx, cy):
        return chip_at(cx, cy) * 2 + core

    flights = {}

    class Flight:
        def __init__(self, key, copy):
            self.key, self.copy = key, copy

        def start(self):
            flights[self.key] = [self.copy, False]
            self.copy.start()

        def wait_recv(self):
            flights[self.key][1] = True
            self.copy.wait_recv()

    def remote(key, src, dst, ssem, rsem, dev):
        copy = pltpu.make_async_remote_copy(
            src_ref=src, dst_ref=dst, send_sem=ssem, recv_sem=rsem, device_id=dev, device_id_type=MESH
        )
        return Flight(key, copy)

    def settle():
        for copy, seen in flights.values():
            if not seen:
                copy.wait_recv()
            copy.wait_send()

    def block(h, da, db):
        return chip_at(x + da, y + db) if h == 0 else chip_at(x + db, y + da)

    def near(h, axis, step):
        if (axis == 0) == (h == 0):
            return {"tp": tp_at(x + step, y)}
        return {"tp": tp_at(x, y + step)}

    def small_block(da, db):
        return chip_at(x + da + core * (db - da), y + db + core * (da - db))

    def small_near(da, db):
        return {"tp": small_block(da, db) * 2 + core}

    first = core == 0
    own_feat = pl.ds(pl.multiple_of(core * HEADW, HEADW), HEADW)
    oth_feat = pl.ds(pl.multiple_of((1 - core) * HEADW, HEADW), HEADW)

    def tokens(half, q):
        return pl.ds(pl.multiple_of(half * HALF + q * QUART, QUART), QUART)

    def w_rows(p):
        return pl.ds(pl.multiple_of(p * LANES + core * HEADW, HEADW), HEADW)

    load_x = [
        pltpu.make_async_copy(res.at[:, tokens(core, q)], xg.at[chip, q, own_feat], xlsem.at[q]) for q in range(4)
    ]
    load_w = [pltpu.make_async_copy(wqkv.at[p], wraw.at[w_rows(p)], xlsem.at[4 + p]) for p in range(3)]
    load_o = pltpu.make_async_copy(wout, wo.at[own_feat], lsem.at[0])
    load_fi = pltpu.make_async_copy(ffi, fi, lsem.at[1])
    load_fo = pltpu.make_async_copy(ffo, fo, lsem.at[2])
    for copy in load_x + load_w:
        copy.start()
    load_o.start()

    other = tp + 1 - 2 * core
    prev_dev = {"seq": lax.rem(z + 3 + core, 4), "tp": other}
    next_dev = {"seq": lax.rem(z + core, 4), "tp": other}
    z_peer = {"seq": lax.rem(z + 3 + 2 * core, 4), "tp": other}
    barrier = pltpu.get_barrier_semaphore()
    peers = [near(0, 0, 1), near(0, 0, -1), near(0, 1, 1), near(0, 1, -1), partner, z_peer]
    for dev in peers:
        pl.semaphore_signal(barrier, inc=1, device_id=dev, device_id_type=MESH)
    pl.semaphore_wait(barrier, len(peers))

    swap_x = [
        remote(("x", q), res.at[:, tokens(1 - core, q)], xg.at[chip, q, own_feat], xsend.at[q], xrecv.at[q], partner)
        for q in range(4)
    ]
    swap_w = [
        remote(("w", p), wqkv.at[p], wraw.at[w_rows(p)], xsend.at[4 + p], xrecv.at[4 + p], partner) for p in range(3)
    ]
    swap_o = remote("o", wout, wo.at[own_feat], psend.at[0], precv.at[0], partner)
    for copy in swap_x + swap_w:
        copy.start()
    swap_o.start()

    def quarters(h, part):
        return pl.ds(2 * h, 2) if part is None else pl.ds(2 * h + part, 1)

    def g_item(h, item, d):
        s = SIGN[d]
        index, part, axis = {
            0: (block(h, 0, 0), None, 0),
            1: (block(h, 0, 0), None, 1),
            2: (block(h, -s, 0), d, 0),
            3: (block(h, -1, 0), None, 1),
            4: (block(h, 1, 0), None, 1),
            5: (block(h, 0, -s), d, 1),
            6: (block(h, 2, 0), None, 1),
            7: (block(h, -1, -s), d, 1),
            8: (block(h, 1, -s), d, 1),
            9: (block(h, 2, -s), d, 1),
        }[item]
        src = xg.at[index, quarters(h, part)]
        return remote(("g", h, item, d), src, src, gsend.at[h, item, d], grecv.at[h, item, d], near(h, axis, s))

    both_hd = [(h, d) for h in range(2) for d in range(2)]

    def g_start(item):
        for h, d in both_hd:
            g_item(h, item, d).start()

    def g_wait(item):
        for h, d in both_hd:
            g_item(h, item, d).wait_recv()

    for h in range(2):
        for q in (2 * h, 2 * h + 1):
            load_x[q].wait()
            swap_x[q].wait_recv()
        for d in range(2):
            g_item(h, 0, d).start()
    g_start(1)
    load_fi.start()
    load_fo.start()

    for p in range(3):
        load_w[p].wait()
        swap_w[p].wait_recv()
    for k in range(CHIPS):
        cols = slice(k * LANES, (k + 1) * LANES)
        w2[k] = (wraw[:, cols].astype(F32) * gain_a[cols].astype(F32).reshape(1, LANES)).astype(BF16)

    g_wait(0)
    g_start(2)
    g_start(3)
    g_start(4)

    acc[...] = jnp.zeros_like(acc)
    ssq[...] = jnp.zeros_like(ssq)

    def qkv_pair(i1, i2):
        wpair = jnp.concatenate([w2[i1], w2[i2]], axis=1)

        def step(q, carry):
            xx = jnp.concatenate([xg[i1, q], xg[i2, q]], axis=0)
            acc[q] += dot(wpair, xx)
            f = xx.astype(F32)
            ssq[q] += jnp.sum((f * f).reshape(2 * LANES // 8, 8, QUART), axis=0)
            return carry

        lax.fori_loop(0, 4, step, 0)

    row = route[...].astype(F32)
    r_i = lax.broadcasted_iota(jnp.int32, (CAP, CAP), 0)
    c_i = lax.broadcasted_iota(jnp.int32, (CAP, CAP), 1)
    col = jnp.sum(jnp.where(r_i == c_i, row, 0.0), axis=1, keepdims=True) - (core * HALF).astype(F32)
    lane = lax.broadcasted_iota(jnp.int32, (CAP, HALF), 1).astype(F32)
    oh[...] = jnp.where(lane == col, 1.0, 0.0).astype(BF16)
    k_i = lax.broadcasted_iota(jnp.int32, (3 * QBLK, QBLK), 0) - QBLK
    q_i = lax.broadcasted_iota(jnp.int32, (3 * QBLK, QBLK), 1)
    band = jnp.where(jnp.abs(q_i - k_i) <= RADIUS, 0.0, NEG)
    bias[0] = band + jnp.where(k_i < 0, jnp.where(z + core == 0, NEG, 0.0), 0.0)
    bias[1] = band
    bias[2] = band + jnp.where(k_i >= QBLK, jnp.where(z + core == 4, NEG, 0.0), 0.0)
    load_o.wait()
    swap_o.wait_recv()
    for k in range(CHIPS):
        at = slice(k * LANES, (k + 1) * LANES)
        wot[at] = wo[:, at].astype(F32).T.astype(BF16)

    g_wait(1)
    g_start(5)
    qkv_pair(chip_at(x - 1, y), chip_at(x + 1, y))
    g_wait(2)
    g_start(6)
    qkv_pair(chip_at(x, y - 1), chip_at(x, y + 1))
    g_wait(3)
    g_start(7)
    g_wait(4)
    g_start(8)

    mine_r = pl.ds(pl.multiple_of(core * CAPC, 16), CAPC)
    theirs_r = pl.ds(pl.multiple_of((1 - core) * CAPC, 16), CAPC)

    def pick(block_of):
        total = jnp.zeros((CAP, LANES), F32)
        for q in range(4):
            total = total + dot_nt(oh[:, q * QUART : (q + 1) * QUART], block_of(q))
        return total.astype(BF16)

    pk[0] = pick(lambda q: xg[chip, q])
    swap_r = [
        remote(("r", i), pk.at[i, theirs_r], px.at[i], psend.at[1 + i], precv.at[1 + i], partner) for i in range(2)
    ]
    swap_r[0].start()

    g_wait(5)
    qkv_pair(chip_at(x - 1, y - 1), chip_at(x + 1, y - 1))
    qkv_pair(chip_at(x - 1, y + 1), chip_at(x + 1, y + 1))
    g_wait(6)
    g_start(9)
    qkv_pair(chip_at(x + 2, y), chip_at(x, y + 2))
    g_wait(7)
    g_wait(8)
    qkv_pair(chip_at(x + 2, y - 1), chip_at(x + 2, y + 1))
    qkv_pair(chip_at(x - 1, y + 2), chip_at(x + 1, y + 2))
    g_wait(9)
    qkv_pair(chip, chip_at(x + 2, y + 2))

    def finish_qkv(q):
        scale = lax.rsqrt(jnp.sum(ssq[q], axis=0, keepdims=True) * (1.0 / FEAT) + EPS)
        qt[:, q * QUART : (q + 1) * QUART] = (
            (acc[q, 0:LANES] * scale).astype(BF16).astype(F32) * (1.0 / HEADW**0.5)
        ).astype(BF16)
        keys = (acc[q, LANES : 2 * LANES] * scale).T.astype(BF16)
        vals = (acc[q, 2 * LANES :] * scale).astype(BF16)
        for half in range(2):
            at = slice(half * QBLK, (half + 1) * QBLK)
            kvb[1 + 2 * q + half, 0] = keys[at]
            kvb[1 + 2 * q + half, 1] = vals[:, at]

    h_prev = remote("hp", kvb.at[1], kvb.at[NBLK + 1], hsend.at[0], hrecv.at[0], prev_dev)
    h_next = remote("hn", kvb.at[NBLK], kvb.at[0], hsend.at[1], hrecv.at[1], next_dev)
    finish_qkv(0)
    finish_qkv(3)
    h_prev.start()
    h_next.start()
    finish_qkv(1)
    finish_qkv(2)

    def attend(i, kind):
        at = pl.ds(pl.multiple_of(i * QBLK, QBLK), QBLK)
        q = qt[:, at]
        zero = jnp.zeros((HEADW, QBLK), BF16)
        q2 = jnp.concatenate(
            [jnp.concatenate([q[:HEADW], zero], axis=0), jnp.concatenate([zero, q[HEADW:]], axis=0)], axis=1
        )
        keys = jnp.concatenate([kvb[i, 0], kvb[i + 1, 0], kvb[i + 2, 0]], axis=0)
        vals = jnp.concatenate([kvb[i, 1], kvb[i + 1, 1], kvb[i + 2, 1]], axis=1)
        b = bias[kind]
        s = dot(keys, q2) + jnp.concatenate([b, b], axis=1)
        e = jnp.exp(s - jnp.max(s, axis=0, keepdims=True))
        total = jnp.sum(e, axis=0, keepdims=True)
        o = dot(vals, e.astype(BF16)) / total
        ctx[:, at] = jnp.concatenate([o[:HEADW, :QBLK], o[HEADW:, QBLK:]], axis=0).astype(BF16)

    def attend_mid(i, carry):
        attend(i, 1)
        return carry

    lax.fori_loop(1, NBLK - 1, attend_mid, 0)
    h_prev.wait_recv()
    h_next.wait_recv()
    attend(0, 0)
    attend(NBLK - 1, 2)

    def wot_rows(index):
        return wot[pl.ds(pl.multiple_of(index * LANES, LANES), LANES), :]

    def project(step):
        for h in range(2):
            rhs = ctx[:, 2 * h * QUART : 2 * (h + 1) * QUART]
            for pair in ((2, -1), (1, 0)):
                i1 = block(h, pair[0], step)
                i2 = block(h, pair[1], step)
                o = dot(jnp.concatenate([wot_rows(i1), wot_rows(i2)], axis=0), rhs).astype(BF16)
                for part in range(2):
                    at = slice(part * QUART, (part + 1) * QUART)
                    pb[i1, 2 * h + part] = o[:LANES, at]
                    pb[i2, 2 * h + part] = o[LANES:, at]

    def r1_copy(h, j, kind, d):
        s = SIGN[d]
        db, part = ((2, d), (s, d), (s, 1 - d))[kind]
        src = pb.at[block(h, OFF[j], db), 2 * h + part]
        return remote(
            ("r1", h, j, kind, d), src, rx1.at[h, j, kind, d], r1send.at[h, j, kind, d], r1recv.at[h, j, kind, d], near(h, 1, s)
        )

    def r2_copy(h, kind, d):
        s = SIGN[d]
        da, part = ((2, d), (s, d), (s, 1 - d))[kind]
        src = pb.at[block(h, da, 0), 2 * h + part]
        return remote(("r2", h, kind, d), src, rx2.at[h, kind, d], r2send.at[h, kind, d], r2recv.at[h, kind, d], near(h, 0, s))

    def r1_start(j, kind):
        for h, d in both_hd:
            r1_copy(h, j, kind, d).start()

    def r2_start(kind):
        for h, d in both_hd:
            r2_copy(h, kind, d).start()

    def relay1(j):
        for h, d in both_hd:
            r1_copy(h, j, 0, d).wait_recv()
            index = block(h, OFF[j], SIGN[d])
            q = 2 * h + d
            pb[index, q] = (pb[index, q].astype(F32) + rx1[h, j, 0, d].astype(F32)).astype(BF16)
            r1_copy(h, j, 1, d).start()

    def relay2():
        for h, d in both_hd:
            r2_copy(h, 0, d).wait_recv()
            index = block(h, SIGN[d], 0)
            q = 2 * h + d
            pb[index, q] = (pb[index, q].astype(F32) + rx2[h, 0, d].astype(F32)).astype(BF16)
            r2_copy(h, 1, d).start()

    def sum1(h, j, part):
        got = pb[block(h, OFF[j], 0), 2 * h + part].astype(F32)
        return got + rx1[h, j, 1, part].astype(F32) + rx1[h, j, 2, 1 - part].astype(F32)

    def wait1(h, j):
        for d in range(2):
            r1_copy(h, j, 1, d).wait_recv()
            r1_copy(h, j, 2, d).wait_recv()

    def total1(j):
        for h in range(2):
            wait1(h, j)
            for part in range(2):
                pb[block(h, OFF[j], 0), 2 * h + part] = sum1(h, j, part).astype(BF16)

    def last():
        for h in range(2):
            wait1(h, 3)
            for d in range(2):
                r2_copy(h, 1, d).wait_recv()
                r2_copy(h, 2, d).wait_recv()
            for part in range(2):
                mixed = sum1(h, 3, part) + rx2[h, 1, part].astype(F32) + rx2[h, 2, 1 - part].astype(F32)
                q = 2 * h + part
                upd[q] = (xg[chip, q].astype(F32) + mixed).astype(BF16)

    def s1_copy(n, t, j):
        src = sb.at[n, small_block(t, j)]
        return remote(("s1", n, t, j), src, rxa.at[n, t - 1, j], s1send.at[n, t - 1, j], s1recv.at[n, t - 1, j], small_near(t, 0))

    def s2_copy(n, t):
        src = sb2.at[n, t]
        return remote(("s2", n, t), src, rxb.at[n, t - 1], s2send.at[n, t - 1], s2recv.at[n, t - 1], small_near(0, t))

    STEPS = (2, 1, 3)
    COLS = (2, 1, 3, 0)

    def small_start(n):
        for j in COLS:
            for t in STEPS:
                s1_copy(n, t, j).start()

    def small_mid(n):
        for j in COLS:
            total = sb[n, small_block(0, j)].astype(F32)
            for t in STEPS:
                s1_copy(n, t, j).wait_recv()
                total = total + rxa[n, t - 1, j].astype(F32)
            sb2[n, j] = total.astype(BF16)
            if j > 0:
                s2_copy(n, j).start()

    def small_end(n):
        total = sb2[n, 0].astype(F32)
        for t in STEPS:
            s2_copy(n, t).wait_recv()
            total = total + rxb[n, t - 1].astype(F32)
        return total

    def a_copy(t, j):
        if t == 0:
            src = gp.at[chip, mine_r]
            return remote(("a", 0, j), src, src, asend.at[0, j], arecv.at[0, j], small_near(0, j))
        src = gp.at[small_block(0, -j), mine_r]
        return remote(("a", t, j), src, src, asend.at[t, j], arecv.at[t, j], small_near(t, 0))

    def f_copy(t, j):
        src = gp.at[small_block(-t, -j), mine_r]
        return remote(("f", t, j), src, src, fsend.at[t, j], frecv.at[t, j], partner)

    def gather_first():
        for j in STEPS:
            a_copy(0, j).start()
        for t in STEPS:
            a_copy(t, 0).start()
        f_copy(0, 0).start()

    def gather_second():
        for j in (1, 3, 2):
            a_copy(0, j).wait_recv()
            for t in STEPS:
                a_copy(t, j).start()
            f_copy(0, j).start()

    def gather_third():
        for j in (0, 1, 3, 2):
            for t in (1, 3, 2):
                a_copy(t, j).wait_recv()
                f_copy(t, j).start()

    def gather_last():
        for j in range(SIDE):
            for t in range(SIDE):
                f_copy(t, j).wait_recv()

    pk[1] = pick(lambda q: ctx[:, q * QUART : (q + 1) * QUART])
    swap_r[1].start()
    project(2)
    r1_start(0, 0)
    swap_r[0].wait_recv()
    swap_r[1].wait_recv()
    rows_ctx = (pk[1, mine_r].astype(F32) + px[1].astype(F32)).astype(BF16)
    for k in range(CHIPS // 2):
        o = dot(rows_ctx, wo[:, k * 256 : (k + 1) * 256]).astype(BF16)
        sb[0, 2 * k] = o[:, :LANES]
        sb[0, 2 * k + 1] = o[:, LANES:]
    small_start(0)
    project(1)
    project(-1)
    r1_start(0, 2)
    small_mid(0)
    r1_start(1, 0)
    relay1(0)
    rows_new = pk[0, mine_r].astype(F32) + px[0].astype(F32) + small_end(0)
    gp[chip, mine_r] = rows_new.astype(BF16)
    gather_first()
    r1_start(2, 0)
    project(0)
    gather_second()
    r1_start(1, 2)
    relay1(1)
    gather_third()
    r1_start(2, 2)
    r1_start(3, 0)
    relay1(2)
    total1(0)
    r2_start(0)
    gather_last()

    sq = jnp.zeros((CAP, LANES), F32)
    for k in range(CHIPS):
        v = gp[k].astype(F32)
        sq = sq + v * v
    scale = lax.rsqrt(jnp.sum(sq, axis=1, keepdims=True) * (1.0 / FEAT) + EPS)
    for k in range(CHIPS):
        at = slice(k * LANES, (k + 1) * LANES)
        nrm[:, at] = (gp[k].astype(F32) * scale * gain_f[at].astype(F32).reshape(1, LANES)).astype(BF16)

    r1_start(3, 2)
    load_fi.wait()

    def ffn_in(n0, nw):
        rows_n = nrm[...]
        gate = dot(rows_n, fi[0, :, n0 : n0 + nw])
        up = dot(rows_n, fi[1, :, n0 : n0 + nw])
        hid[:, n0 : n0 + nw] = (gelu(gate) * up).astype(BF16)

    ffn_in(0, 256)
    total1(1)
    total1(2)
    r2_start(2)
    ffn_in(256, 256)
    relay1(3)
    ffn_in(512, 128)
    relay2()
    load_fo.wait()

    def c_copy(n):
        pair = pl.ds(2 * n, 2)
        return remote(("c", n), pb2.at[pair, theirs_r], rxc.at[pair], csend.at[n], crecv.at[n], partner)

    for n in range(CHIPS // 2):
        o = dot(hid[...], fo[:, n * 256 : (n + 1) * 256]).astype(BF16)
        pb2[2 * n] = o[:, :LANES]
        pb2[2 * n + 1] = o[:, LANES:]
        c_copy(n).start()
    for n in range(CHIPS // 2):
        c_copy(n).wait_recv()
        for k in (2 * n, 2 * n + 1):
            sb[1, k] = (pb2[k, mine_r].astype(F32) + rxc[k].astype(F32)).astype(BF16)
    small_start(1)
    last()
    small_mid(1)
    heavy = small_end(1)
    slot = lax.broadcasted_iota(jnp.int32, (CAPC, LANES), 0) + core * CAPC
    heavy = jnp.where(slot < counts[z], heavy, 0.0)
    high = heavy.astype(BF16)
    hv[mine_r, 0:LANES] = high
    hv[mine_r, LANES:] = (heavy - high.astype(F32)).astype(BF16)
    swap_h = remote("h", hv.at[mine_r], hv.at[mine_r], psend.at[3], precv.at[3], partner)
    swap_h.start()
    swap_h.wait_recv()

    for q in range(4):
        at = slice(q * QUART, (q + 1) * QUART)
        added = dot_tn(hv[...], oh[:, at])
        fin[:, at] = (upd[q].astype(F32) + added[:LANES] + added[LANES:]).astype(BF16)
    out_part = out.at[:, pl.ds(pl.multiple_of(core * HALF, HALF), HALF)]
    send_out = remote("out", fin.at[oth_feat], out_part, psend.at[4], precv.at[4], partner)
    send_out.start()
    save_out = pltpu.make_async_copy(fin.at[own_feat], out_part, lsem.at[3])
    save_out.start()

    save_out.wait()
    settle()


def local(
    residual, attn_gain, attn_in, attn_out, ffn_gain, ffn_in, ffn_out, route_rows, route_counts
):
    any_spec = pl.BlockSpec(memory_space=pl.ANY)
    vm = pltpu.VMEM
    dma = pltpu.SemaphoreType.DMA
    turned = pl.pallas_call(
        kernel,
        out_shape=jax.ShapeDtypeStruct((HEADW, TOK), BF16),
        in_specs=[any_spec] * 5
        + [pl.BlockSpec(memory_space=pltpu.VMEM)] * 3
        + [pl.BlockSpec(memory_space=pltpu.SMEM)],
        out_specs=any_spec,
        scratch_shapes=[
            vm((3 * LANES, FEAT), BF16),
            vm((LANES, FEAT), BF16),
            vm((FEAT, LANES), BF16),
            vm((2, FEAT, FFU), BF16),
            vm((FFU, FEAT), BF16),
            vm((CHIPS, 3 * LANES, LANES), BF16),
            vm((CHIPS, 4, LANES, QUART), BF16),
            vm((4, 3 * LANES, QUART), F32),
            vm((4, 8, QUART), F32),
            vm((LANES, HALF), BF16),
            vm((NBLK + 2, 2, QBLK, QBLK), BF16),
            vm((LANES, HALF), BF16),
            vm((3, 3 * QBLK, QBLK), F32),
            vm((CAP, HALF), BF16),
            vm((CHIPS, 4, LANES, QUART), BF16),
            vm((2, 4, 3, 2, LANES, QUART), BF16),
            vm((2, 3, 2, LANES, QUART), BF16),
            vm((4, LANES, QUART), BF16),
            vm((LANES, HALF), BF16),
            vm((CHIPS, CAP, LANES), BF16),
            vm((2, CAP, LANES), BF16),
            vm((2, CAPC, LANES), BF16),
            vm((CAP, FEAT), BF16),
            vm((CAP, FFU), BF16),
            vm((CHIPS, CAP, LANES), BF16),
            vm((CHIPS, CAPC, LANES), BF16),
            vm((2, CHIPS, CAPC, LANES), BF16),
            vm((2, 3, SIDE, CAPC, LANES), BF16),
            vm((2, SIDE, CAPC, LANES), BF16),
            vm((2, 3, CAPC, LANES), BF16),
            vm((CAP, 2 * LANES), BF16),
            dma((4,)),
            dma((7,)),
            dma((7,)),
            dma((7,)),
            dma((5,)),
            dma((5,)),
            dma((2, 10, 2)),
            dma((2, 10, 2)),
            dma((2,)),
            dma((2,)),
            dma((2, 4, 3, 2)),
            dma((2, 4, 3, 2)),
            dma((2, 3, 2)),
            dma((2, 3, 2)),
            dma((2, 3, SIDE)),
            dma((2, 3, SIDE)),
            dma((2, 3)),
            dma((2, 3)),
            dma((SIDE, SIDE)),
            dma((SIDE, SIDE)),
            dma((SIDE, SIDE)),
            dma((SIDE, SIDE)),
            dma((CHIPS // 2,)),
            dma((CHIPS // 2,)),
        ],
        compiler_params=pltpu.CompilerParams(
            collective_id=0, has_side_effects=True, vmem_limit_bytes=62 * 1024 * 1024
        ),
        name="layer",
    )(
        residual.T, attn_in.transpose(0, 2, 1), attn_out, ffn_in, ffn_out, attn_gain, ffn_gain, route_rows, route_counts
    )
    return turned.T


def solution(mesh):
    in_specs = (
        P("seq", "tp"),
        P(),
        P(None, None, "tp"),
        P("tp", None),
        P(),
        P(None, None, "tp"),
        P("tp", None),
        P("seq", None),
        P(),
    )
    out_specs = P("seq", "tp")
    return jax.shard_map(local, mesh=mesh, in_specs=in_specs, out_specs=out_specs, check_vma=False)
```

time: 335 us -> 85.4 us (0.25)
  waiting for transfers between devices: 224 us -> 0 us
  Pallas kernels: 0 us -> 83.5 us
  matrix products: 31.4 us -> 0 us
  blocking collectives: 26.7 us -> 0 us
  other arithmetic: 14.5 us -> 0 us
  local copies, waits for them, and re-layouts: 15.5 us -> 1.67 us
  between operations: 13.3 us -> 0.01 us
  starting transfers between devices: 4.56 us -> 0 us
    reduce_scatter x2 -> x0, waiting for transfers between devices: 162 us -> none  [the longest x1 90.7 us: local(): lax.psum_scatter(partial_mix.astype(jnp.bfloat16), 'tp', scatter_dimensio...]
    pallas_call x0 -> x1, Pallas kernels: none -> 83.5 us  [local(): pl.pallas_call(kernel, out_shape=jax.ShapeDtypeStruct((HEADW, TOK), BF16)...]
    all_gather x1 -> x0, waiting for transfers between devices: 57.8 us -> none  [local(): whole = lax.all_gather(residual, 'tp', axis=1, tiled=True)]
    dot_general x11 -> x0, matrix products: 27.8 us -> none  [the longest x4 8.49 us: attend(): jnp.einsum('hqk,khd->qhd', prob_rows, value_blk, preferred_element_type=j...]
    all_gather x1 -> x0, blocking collectives: 26.7 us -> none  [heavy_branch(): full_rows = lax.all_gather(rows_part, 'tp', axis=1, tiled=True)]
    reduce_sum x6 -> x0, other arithmetic: 7.15 us -> none  [the longest x2 5.6 us: rms_norm(): mean_square = jnp.mean(wide * wide, axis=-1, keepdims=True)]
    while x8 -> x0, local copies, waits for them, and re-layouts: 4.67 us -> none
    ppermute x2 -> x0, starting transfers between devices: 4.48 us -> none  [the longest x1 3.19 us: extended(): lax.ppermute(lax.slice_in_dim(block, block.shape[dim] - width, None, axis...]
  transfers between devices with their start and end apart: 5 -> 0, of which waited for: 4 -> 0; matrix products, arithmetic and copies ran while one was open for 1% -> 0% of each run, Pallas kernels for 0% -> 0%
where the time goes in v2:
time: 85.4 us; the launch traced here: 85.2 us
  Pallas kernels  83.5 us (98%)
  local copies, waits for them, and re-layouts  1.67 us (2%)
    pallas_call x1, Pallas kernels, local(): pl.pallas_call(kernel, out_shape=jax.ShapeDtypeStruct((HEADW, TOK), BF16)...  83.5 us

profile of v2, /device:TPU:1, one launch (start us, length us, event | category | flops | bytes accessed | tf_op | source)
XLA Modules:
  0.0 85.2 jit_solution(4327369901661420307)
XLA Ops:
  0.0 83.5 %layer.1 = bf16[64,2048]{1,0:T(8,128)(2,1)} custom-call(bf16[64,2048]{1,0:T(8,128)(2,1)} %bitcast.5, bf16[3,64,2048]{2,1,0:T(8,128)(2,1)} %bitcast.4, bf16[64,2048]{1,0:T(8,128)(2,1)} %wout.1, bf16[2,2048,640]{2,1,0:T(8,128)(2,1)} %ffi.1, bf16[640,2048]{1,0:T(8,128)(2,1)} %ffo.1, bf16[2048]{0:T(1024)(128)(2,1)} %gain_a.1, bf16[2048]{0:T(1024)(128)(2,1)} %gain_f.1, ...), custom_call_target="tpu_custom_call" | custom-call | tf_op jit(solution)/shard_map/layer/pallas_call | solution.py:583
  83.6 1.7 %copy.11 = bf16[2048,64]{0,1:T(8,128)(2,1)} copy(bf16[2048,64]{0,1:T(8,128)(2,1)} %bitcast.3) | data formatting | bytes 524288

commit v3 on v2

--- a/solution.py
+++ b/solution.py
@@ -49,9 +49,7 @@
     out,
     wraw, wo, wot, fi, fo, w2, xg, acc, ssq, qt, kvb, ctx, bias, oh,
     pb, rx1, rx2, upd, fin, gp, pk, px, nrm, hid, pb2, rxc, sb, rxa, sb2, rxb, hv,
-    lsem, xlsem, xsend, xrecv, psend, precv, gsend, grecv, hsend, hrecv,
-    r1send, r1recv, r2send, r2recv, s1send, s1recv, s2send, s2recv,
-    asend, arecv, fsend, frecv, csend, crecv,
+    loads, sends, recvs, grecv, rrecv, s1recv, s2recv, arecv, crecv,
 ):
     z = lax.axis_index("seq")
     tp = lax.axis_index("tp")
@@ -70,31 +68,16 @@
     def tp_at(cx, cy):
         return chip_at(cx, cy) * 2 + core
 
-    flights = {}
-
-    class Flight:
-        def __init__(self, key, copy):
-            self.key, self.copy = key, copy
-
-        def start(self):
-            flights[self.key] = [self.copy, False]
-            self.copy.start()
-
-        def wait_recv(self):
-            flights[self.key][1] = True
-            self.copy.wait_recv()
-
-    def remote(key, src, dst, ssem, rsem, dev):
-        copy = pltpu.make_async_remote_copy(
+    def remote(src, dst, ssem, rsem, dev):
+        return pltpu.make_async_remote_copy(
             src_ref=src, dst_ref=dst, send_sem=ssem, recv_sem=rsem, device_id=dev, device_id_type=MESH
         )
-        return Flight(key, copy)
-
-    def settle():
-        for copy, seen in flights.values():
-            if not seen:
-                copy.wait_recv()
-            copy.wait_send()
+
+    def arrived(sem, ref):
+        remote(ref, ref, sends.at[0], sem, partner).wait_recv()
+
+    def left(n, ref):
+        remote(ref, ref, sends.at[n], recvs.at[0], partner).wait_send()
 
     def block(h, da, db):
         return chip_at(x + da, y + db) if h == 0 else chip_at(x + db, y + da)
@@ -121,12 +104,12 @@
         return pl.ds(pl.multiple_of(p * LANES + core * HEADW, HEADW), HEADW)
 
     load_x = [
-        pltpu.make_async_copy(res.at[:, tokens(core, q)], xg.at[chip, q, own_feat], xlsem.at[q]) for q in range(4)
+        pltpu.make_async_copy(res.at[:, tokens(core, q)], xg.at[chip, q, own_feat], loads.at[0]) for q in range(4)
     ]
-    load_w = [pltpu.make_async_copy(wqkv.at[p], wraw.at[w_rows(p)], xlsem.at[4 + p]) for p in range(3)]
-    load_o = pltpu.make_async_copy(wout, wo.at[own_feat], lsem.at[0])
-    load_fi = pltpu.make_async_copy(ffi, fi, lsem.at[1])
-    load_fo = pltpu.make_async_copy(ffo, fo, lsem.at[2])
+    load_w = [pltpu.make_async_copy(wqkv.at[p], wraw.at[w_rows(p)], loads.at[1]) for p in range(3)]
+    load_o = pltpu.make_async_copy(wout, wo.at[own_feat], loads.at[2])
+    load_fi = pltpu.make_async_copy(ffi, fi, loads.at[3])
+    load_fo = pltpu.make_async_copy(ffo, fo, loads.at[4])
     for copy in load_x + load_w:
         copy.start()
     load_o.start()
@@ -142,13 +125,13 @@
     pl.semaphore_wait(barrier, len(peers))
 
     swap_x = [
-        remote(("x", q), res.at[:, tokens(1 - core, q)], xg.at[chip, q, own_feat], xsend.at[q], xrecv.at[q], partner)
+        remote(res.at[:, tokens(1 - core, q)], xg.at[chip, q, own_feat], sends.at[0], recvs.at[q // 2], partner)
         for q in range(4)
     ]
     swap_w = [
-        remote(("w", p), wqkv.at[p], wraw.at[w_rows(p)], xsend.at[4 + p], xrecv.at[4 + p], partner) for p in range(3)
+        remote(wqkv.at[p], wraw.at[w_rows(p)], sends.at[1], recvs.at[2], partner) for p in range(3)
     ]
-    swap_o = remote("o", wout, wo.at[own_feat], psend.at[0], precv.at[0], partner)
+    swap_o = remote(wout, wo.at[own_feat], sends.at[2], recvs.at[3], partner)
     for copy in swap_x + swap_w:
         copy.start()
     swap_o.start()
@@ -156,7 +139,7 @@
     def quarters(h, part):
         return pl.ds(2 * h, 2) if part is None else pl.ds(2 * h + part, 1)
 
-    def g_item(h, item, d):
+    def g_item(h, item, d, piece=None):
         s = SIGN[d]
         index, part, axis = {
             0: (block(h, 0, 0), None, 0),
@@ -170,8 +153,9 @@
             8: (block(h, 1, -s), d, 1),
             9: (block(h, 2, -s), d, 1),
         }[item]
-        src = xg.at[index, quarters(h, part)]
-        return remote(("g", h, item, d), src, src, gsend.at[h, item, d], grecv.at[h, item, d], near(h, axis, s))
+        feats = {None: pl.ds(0, LANES), 0: own_feat, 1: oth_feat}[piece]
+        src = xg.at[index, quarters(h, part), feats]
+        return remote(src, src, sends.at[3], grecv.at[item], near(h, axis, s))
 
     both_hd = [(h, d) for h in range(2) for d in range(2)]
 
@@ -180,22 +164,23 @@
             g_item(h, item, d).start()
 
     def g_wait(item):
+        arrived(grecv.at[item], xg.at[0:2] if item in (0, 1, 3, 4, 6) else xg.at[0])
+
+    pltpu.make_async_copy(xg.at[0, 0:2], xg.at[0, 0:2], loads.at[0]).wait()
+    for item in range(2):
         for h, d in both_hd:
-            g_item(h, item, d).wait_recv()
-
+            g_item(h, item, d, 0).start()
     for h in range(2):
-        for q in (2 * h, 2 * h + 1):
-            load_x[q].wait()
-            swap_x[q].wait_recv()
+        arrived(recvs.at[h], xg.at[0, 0])
         for d in range(2):
-            g_item(h, 0, d).start()
-    g_start(1)
+            g_item(h, 0, d, 1).start()
+    for h, d in both_hd:
+        g_item(h, 1, d, 1).start()
     load_fi.start()
     load_fo.start()
 
-    for p in range(3):
-        load_w[p].wait()
-        swap_w[p].wait_recv()
+    pltpu.make_async_copy(wraw.at[0 : 3 * HEADW], wraw.at[0 : 3 * HEADW], loads.at[1]).wait()
+    arrived(recvs.at[2], wraw.at[0 : 3 * HEADW])
     for k in range(CHIPS):
         cols = slice(k * LANES, (k + 1) * LANES)
         w2[k] = (wraw[:, cols].astype(F32) * gain_a[cols].astype(F32).reshape(1, LANES)).astype(BF16)
@@ -233,7 +218,7 @@
     bias[1] = band
     bias[2] = band + jnp.where(k_i >= QBLK, jnp.where(z + core == 4, NEG, 0.0), 0.0)
     load_o.wait()
-    swap_o.wait_recv()
+    arrived(recvs.at[3], wo.at[0:HEADW])
     for k in range(CHIPS):
         at = slice(k * LANES, (k + 1) * LANES)
         wot[at] = wo[:, at].astype(F32).T.astype(BF16)
@@ -260,7 +245,7 @@
 
     pk[0] = pick(lambda q: xg[chip, q])
     swap_r = [
-        remote(("r", i), pk.at[i, theirs_r], px.at[i], psend.at[1 + i], precv.at[1 + i], partner) for i in range(2)
+        remote(pk.at[i, theirs_r], px.at[i], sends.at[4], recvs.at[4 + i], partner) for i in range(2)
     ]
     swap_r[0].start()
 
@@ -289,8 +274,8 @@
             kvb[1 + 2 * q + half, 0] = keys[at]
             kvb[1 + 2 * q + half, 1] = vals[:, at]
 
-    h_prev = remote("hp", kvb.at[1], kvb.at[NBLK + 1], hsend.at[0], hrecv.at[0], prev_dev)
-    h_next = remote("hn", kvb.at[NBLK], kvb.at[0], hsend.at[1], hrecv.at[1], next_dev)
+    h_prev = remote(kvb.at[1], kvb.at[NBLK + 1], sends.at[5], recvs.at[6], prev_dev)
+    h_next = remote(kvb.at[NBLK], kvb.at[0], sends.at[5], recvs.at[7], next_dev)
     finish_qkv(0)
     finish_qkv(3)
     h_prev.start()
@@ -319,8 +304,8 @@
         return carry
 
     lax.fori_loop(1, NBLK - 1, attend_mid, 0)
-    h_prev.wait_recv()
-    h_next.wait_recv()
+    arrived(recvs.at[6], kvb.at[0])
+    arrived(recvs.at[7], kvb.at[0])
     attend(0, 0)
     attend(NBLK - 1, 2)
 
@@ -343,15 +328,13 @@
         s = SIGN[d]
         db, part = ((2, d), (s, d), (s, 1 - d))[kind]
         src = pb.at[block(h, OFF[j], db), 2 * h + part]
-        return remote(
-            ("r1", h, j, kind, d), src, rx1.at[h, j, kind, d], r1send.at[h, j, kind, d], r1recv.at[h, j, kind, d], near(h, 1, s)
-        )
+        return remote(src, rx1.at[h, j, kind, d], sends.at[6], rrecv.at[j if kind == 0 else 4 + j], near(h, 1, s))
 
     def r2_copy(h, kind, d):
         s = SIGN[d]
         da, part = ((2, d), (s, d), (s, 1 - d))[kind]
         src = pb.at[block(h, da, 0), 2 * h + part]
-        return remote(("r2", h, kind, d), src, rx2.at[h, kind, d], r2send.at[h, kind, d], r2recv.at[h, kind, d], near(h, 0, s))
+        return remote(src, rx2.at[h, kind, d], sends.at[6], rrecv.at[8 if kind == 0 else 9], near(h, 0, s))
 
     def r1_start(j, kind):
         for h, d in both_hd:
@@ -362,16 +345,16 @@
             r2_copy(h, kind, d).start()
 
     def relay1(j):
+        arrived(rrecv.at[j], xg.at[0])
         for h, d in both_hd:
-            r1_copy(h, j, 0, d).wait_recv()
             index = block(h, OFF[j], SIGN[d])
             q = 2 * h + d
             pb[index, q] = (pb[index, q].astype(F32) + rx1[h, j, 0, d].astype(F32)).astype(BF16)
             r1_copy(h, j, 1, d).start()
 
     def relay2():
+        arrived(rrecv.at[8], xg.at[0])
         for h, d in both_hd:
-            r2_copy(h, 0, d).wait_recv()
             index = block(h, SIGN[d], 0)
             q = 2 * h + d
             pb[index, q] = (pb[index, q].astype(F32) + rx2[h, 0, d].astype(F32)).astype(BF16)
@@ -381,23 +364,16 @@
         got = pb[block(h, OFF[j], 0), 2 * h + part].astype(F32)
         return got + rx1[h, j, 1, part].astype(F32) + rx1[h, j, 2, 1 - part].astype(F32)
 
-    def wait1(h, j):
-        for d in range(2):
-            r1_copy(h, j, 1, d).wait_recv()
-            r1_copy(h, j, 2, d).wait_recv()
-
     def total1(j):
+        arrived(rrecv.at[4 + j], xg.at[0:2])
         for h in range(2):
-            wait1(h, j)
             for part in range(2):
                 pb[block(h, OFF[j], 0), 2 * h + part] = sum1(h, j, part).astype(BF16)
 
     def last():
+        arrived(rrecv.at[7], xg.at[0:2])
+        arrived(rrecv.at[9], xg.at[0:2])
         for h in range(2):
-            wait1(h, 3)
-            for d in range(2):
-                r2_copy(h, 1, d).wait_recv()
-                r2_copy(h, 2, d).wait_recv()
             for part in range(2):
                 mixed = sum1(h, 3, part) + rx2[h, 1, part].astype(F32) + rx2[h, 2, 1 - part].astype(F32)
                 q = 2 * h + part
@@ -405,11 +381,11 @@
 
     def s1_copy(n, t, j):
         src = sb.at[n, small_block(t, j)]
-        return remote(("s1", n, t, j), src, rxa.at[n, t - 1, j], s1send.at[n, t - 1, j], s1recv.at[n, t - 1, j], small_near(t, 0))
+        return remote(src, rxa.at[n, t - 1, j], sends.at[7], s1recv.at[n, j], small_near(t, 0))
 
     def s2_copy(n, t):
         src = sb2.at[n, t]
-        return remote(("s2", n, t), src, rxb.at[n, t - 1], s2send.at[n, t - 1], s2recv.at[n, t - 1], small_near(0, t))
+        return remote(src, rxb.at[n, t - 1], sends.at[7], s2recv.at[n], small_near(0, t))
 
     STEPS = (2, 1, 3)
     COLS = (2, 1, 3, 0)
@@ -422,8 +398,8 @@
     def small_mid(n):
         for j in COLS:
             total = sb[n, small_block(0, j)].astype(F32)
+            arrived(s1recv.at[n, j], sb.at[n, 0:3])
             for t in STEPS:
-                s1_copy(n, t, j).wait_recv()
                 total = total + rxa[n, t - 1, j].astype(F32)
             sb2[n, j] = total.astype(BF16)
             if j > 0:
@@ -431,21 +407,21 @@
 
     def small_end(n):
         total = sb2[n, 0].astype(F32)
+        arrived(s2recv.at[n], sb.at[n, 0:3])
         for t in STEPS:
-            s2_copy(n, t).wait_recv()
             total = total + rxb[n, t - 1].astype(F32)
         return total
 
     def a_copy(t, j):
         if t == 0:
             src = gp.at[chip, mine_r]
-            return remote(("a", 0, j), src, src, asend.at[0, j], arecv.at[0, j], small_near(0, j))
+            return remote(src, src, sends.at[8], arecv.at[3 + j], small_near(0, j))
         src = gp.at[small_block(0, -j), mine_r]
-        return remote(("a", t, j), src, src, asend.at[t, j], arecv.at[t, j], small_near(t, 0))
+        return remote(src, src, sends.at[8], arecv.at[j], small_near(t, 0))
 
     def f_copy(t, j):
         src = gp.at[small_block(-t, -j), mine_r]
-        return remote(("f", t, j), src, src, fsend.at[t, j], frecv.at[t, j], partner)
+        return remote(src, src, sends.at[9], recvs.at[8], partner)
 
     def gather_first():
         for j in STEPS:
@@ -456,28 +432,26 @@
 
     def gather_second():
         for j in (1, 3, 2):
-            a_copy(0, j).wait_recv()
+            arrived(arecv.at[3 + j], sb.at[0, 0])
             for t in STEPS:
                 a_copy(t, j).start()
             f_copy(0, j).start()
 
     def gather_third():
         for j in (0, 1, 3, 2):
+            arrived(arecv.at[j], sb.at[0, 0:3])
             for t in (1, 3, 2):
-                a_copy(t, j).wait_recv()
                 f_copy(t, j).start()
 
     def gather_last():
-        for j in range(SIDE):
-            for t in range(SIDE):
-                f_copy(t, j).wait_recv()
+        arrived(recvs.at[8], sb.at[0])
 
     pk[1] = pick(lambda q: ctx[:, q * QUART : (q + 1) * QUART])
     swap_r[1].start()
     project(2)
     r1_start(0, 0)
-    swap_r[0].wait_recv()
-    swap_r[1].wait_recv()
+    arrived(recvs.at[4], px.at[0])
+    arrived(recvs.at[5], px.at[0])
     rows_ctx = (pk[1, mine_r].astype(F32) + px[1].astype(F32)).astype(BF16)
     for k in range(CHIPS // 2):
         o = dot(rows_ctx, wo[:, k * 256 : (k + 1) * 256]).astype(BF16)
@@ -536,16 +510,16 @@
 
     def c_copy(n):
         pair = pl.ds(2 * n, 2)
-        return remote(("c", n), pb2.at[pair, theirs_r], rxc.at[pair], csend.at[n], crecv.at[n], partner)
+        return remote(pb2.at[pair, theirs_r], rxc.at[pair], sends.at[10], crecv.at[n // 2], partner)
 
     for n in range(CHIPS // 2):
         o = dot(hid[...], fo[:, n * 256 : (n + 1) * 256]).astype(BF16)
         pb2[2 * n] = o[:, :LANES]
         pb2[2 * n + 1] = o[:, LANES:]
         c_copy(n).start()
-    for n in range(CHIPS // 2):
-        c_copy(n).wait_recv()
-        for k in (2 * n, 2 * n + 1):
+    for n in range(4):
+        arrived(crecv.at[n], sb.at[0, 0:4])
+        for k in range(4 * n, 4 * n + 4):
             sb[1, k] = (pb2[k, mine_r].astype(F32) + rxc[k].astype(F32)).astype(BF16)
     small_start(1)
     last()
@@ -556,22 +530,34 @@
     high = heavy.astype(BF16)
     hv[mine_r, 0:LANES] = high
     hv[mine_r, LANES:] = (heavy - high.astype(F32)).astype(BF16)
-    swap_h = remote("h", hv.at[mine_r], hv.at[mine_r], psend.at[3], precv.at[3], partner)
+    swap_h = remote(hv.at[mine_r], hv.at[mine_r], sends.at[11], recvs.at[9], partner)
     swap_h.start()
-    swap_h.wait_recv()
+    arrived(recvs.at[9], hv.at[0:CAPC])
 
     for q in range(4):
         at = slice(q * QUART, (q + 1) * QUART)
         added = dot_tn(hv[...], oh[:, at])
         fin[:, at] = (upd[q].astype(F32) + added[:LANES] + added[LANES:]).astype(BF16)
     out_part = out.at[:, pl.ds(pl.multiple_of(core * HALF, HALF), HALF)]
-    send_out = remote("out", fin.at[oth_feat], out_part, psend.at[4], precv.at[4], partner)
+    send_out = remote(fin.at[oth_feat], out_part, sends.at[12], recvs.at[10], partner)
     send_out.start()
-    save_out = pltpu.make_async_copy(fin.at[own_feat], out_part, lsem.at[3])
+    save_out = pltpu.make_async_copy(fin.at[own_feat], out_part, loads.at[5])
     save_out.start()
 
+    left(0, xg.at[0, 0:2])
+    left(1, wraw.at[0 : 3 * HEADW])
+    left(2, wo.at[0:HEADW])
+    left(3, xg.at[0:15])
+    left(4, px)
+    left(5, kvb.at[0:2])
+    left(6, pb.at[0:15])
+    left(7, sb.at[:, 0:15])
+    left(8, sb.at[0, 0:15])
+    left(9, sb.at[0])
+    left(10, sb.at[1])
+    left(11, hv.at[0:CAPC])
     save_out.wait()
-    settle()
+    send_out.wait()
 
 
 def local(
@@ -619,30 +605,15 @@
             vm((2, SIDE, CAPC, LANES), BF16),
             vm((2, 3, CAPC, LANES), BF16),
             vm((CAP, 2 * LANES), BF16),
+            dma((6,)),
+            dma((13,)),
+            dma((11,)),
+            dma((10,)),
+            dma((10,)),
+            dma((2, SIDE)),
+            dma((2,)),
+            dma((7,)),
             dma((4,)),
-            dma((7,)),
-            dma((7,)),
-            dma((7,)),
-            dma((5,)),
-            dma((5,)),
-            dma((2, 10, 2)),
-            dma((2, 10, 2)),
-            dma((2,)),
-            dma((2,)),
-            dma((2, 4, 3, 2)),
-            dma((2, 4, 3, 2)),
-            dma((2, 3, 2)),
-            dma((2, 3, 2)),
-            dma((2, 3, SIDE)),
-            dma((2, 3, SIDE)),
-            dma((2, 3)),
-            dma((2, 3)),
-            dma((SIDE, SIDE)),
-            dma((SIDE, SIDE)),
-            dma((SIDE, SIDE)),
-            dma((SIDE, SIDE)),
-            dma((CHIPS // 2,)),
-            dma((CHIPS // 2,)),
         ],
         compiler_params=pltpu.CompilerParams(
             collective_id=0, has_side_effects=True, vmem_limit_bytes=62 * 1024 * 1024

time: 85.4 us -> 81.6 us (0.956)
  Pallas kernels: 83.5 us -> 79.8 us
    pallas_call x1, Pallas kernels: 83.5 us -> 79.8 us  [local(): pl.pallas_call(kernel, out_shape=jax.ShapeDtypeStruct((HEADW, TOK), BF16)...]
where the time goes in v3:
time: 81.6 us; the launch traced here: 81.4 us
  Pallas kernels  79.8 us (98%)
  local copies, waits for them, and re-layouts  1.67 us (2%)
    pallas_call x1, Pallas kernels, local(): pl.pallas_call(kernel, out_shape=jax.ShapeDtypeStruct((HEADW, TOK), BF16)...  79.8 us
    unnamed x1, local copies, waits for them, and re-layouts  1.67 us

profile of v3, /device:TPU:1, one launch (start us, length us, event | category | flops | bytes accessed | tf_op | source)
XLA Modules:
  0.0 81.4 jit_solution(16557514071818371368)
XLA Ops:
  0.0 79.8 %layer.1 = bf16[64,2048]{1,0:T(8,128)(2,1)} custom-call(bf16[64,2048]{1,0:T(8,128)(2,1)} %bitcast.5, bf16[3,64,2048]{2,1,0:T(8,128)(2,1)} %bitcast.4, bf16[64,2048]{1,0:T(8,128)(2,1)} %wout.1, bf16[2,2048,640]{2,1,0:T(8,128)(2,1)} %ffi.1, bf16[640,2048]{1,0:T(8,128)(2,1)} %ffo.1, bf16[2048]{0:T(1024)(128)(2,1)} %gain_a.1, bf16[2048]{0:T(1024)(128)(2,1)} %gain_f.1, ...), custom_call_target="tpu_custom_call" | custom-call | tf_op jit(solution)/shard_map/layer/pallas_call | solution.py:569
  79.8 1.7 %copy.11 = bf16[2048,64]{0,1:T(8,128)(2,1)} copy(bf16[2048,64]{0,1:T(8,128)(2,1)} %bitcast.3) | data formatting | bytes 524288

commit v4 on v3

--- a/solution.py
+++ b/solution.py
@@ -26,6 +26,9 @@
 NBLK = HALF // QBLK
 OFF = (2, -1, 1, 0)
 SIGN = (1, -1)
+CHUNK = (((0, 3), (5, 3)), ((3, 1), (4, 1)))
+PAIRS = ((0, 1), (6, 7), (2, 5), (3, 4))
+SETS = ((0, 3), (1, 2))
 
 
 def gelu(v):
@@ -48,7 +51,7 @@
     res, wqkv, wout, ffi, ffo, gain_a, gain_f, route, counts,
     out,
     wraw, wo, wot, fi, fo, w2, xg, acc, ssq, qt, kvb, ctx, bias, oh,
-    pb, rx1, rx2, upd, fin, gp, pk, px, nrm, hid, pb2, rxc, sb, rxa, sb2, rxb, hv,
+    pb, rx1, rx2, upd, fin, gp, pk, px, nrm, hid, pb2, rxc, sb, rxa, sb2, rxb, rxo, hv,
     loads, sends, recvs, grecv, rrecv, s1recv, s2recv, arecv, crecv,
 ):
     z = lax.axis_index("seq")
@@ -97,14 +100,16 @@
     own_feat = pl.ds(pl.multiple_of(core * HEADW, HEADW), HEADW)
     oth_feat = pl.ds(pl.multiple_of((1 - core) * HEADW, HEADW), HEADW)
 
-    def tokens(half, q):
-        return pl.ds(pl.multiple_of(half * HALF + q * QUART, QUART), QUART)
+    def tokens(half, b):
+        return pl.ds(pl.multiple_of(half * HALF + b * QBLK, QBLK), QBLK)
+
+    ORDER = (0, 1, 2, 5, 6, 7, 3, 4)
 
     def w_rows(p):
         return pl.ds(pl.multiple_of(p * LANES + core * HEADW, HEADW), HEADW)
 
     load_x = [
-        pltpu.make_async_copy(res.at[:, tokens(core, q)], xg.at[chip, q, own_feat], loads.at[0]) for q in range(4)
+        pltpu.make_async_copy(res.at[:, tokens(core, b)], xg.at[chip, b, own_feat], loads.at[0]) for b in ORDER
     ]
     load_w = [pltpu.make_async_copy(wqkv.at[p], wraw.at[w_rows(p)], loads.at[1]) for p in range(3)]
     load_o = pltpu.make_async_copy(wout, wo.at[own_feat], loads.at[2])
@@ -125,8 +130,11 @@
     pl.semaphore_wait(barrier, len(peers))
 
     swap_x = [
-        remote(res.at[:, tokens(1 - core, q)], xg.at[chip, q, own_feat], sends.at[0], recvs.at[q // 2], partner)
-        for q in range(4)
+        remote(
+            res.at[:, tokens(1 - core, b)], xg.at[chip, b, own_feat], sends.at[0],
+            recvs.at[1 if b in (3, 4) else 0], partner,
+        )
+        for b in ORDER
     ]
     swap_w = [
         remote(wqkv.at[p], wraw.at[w_rows(p)], sends.at[1], recvs.at[2], partner) for p in range(3)
@@ -136,10 +144,7 @@
         copy.start()
     swap_o.start()
 
-    def quarters(h, part):
-        return pl.ds(2 * h, 2) if part is None else pl.ds(2 * h + part, 1)
-
-    def g_item(h, item, d, piece=None):
+    def g_item(c, h, item, d, piece=None):
         s = SIGN[d]
         index, part, axis = {
             0: (block(h, 0, 0), None, 0),
@@ -153,29 +158,33 @@
             8: (block(h, 1, -s), d, 1),
             9: (block(h, 2, -s), d, 1),
         }[item]
-        feats = {None: pl.ds(0, LANES), 0: own_feat, 1: oth_feat}[piece]
-        src = xg.at[index, quarters(h, part), feats]
-        return remote(src, src, sends.at[3], grecv.at[item], near(h, axis, s))
+        feats = pl.ds(0, LANES) if part is None else pl.ds(part * HEADW, HEADW)
+        if piece is not None:
+            feats = (own_feat, oth_feat)[piece]
+        start, count = CHUNK[c][h]
+        src = xg.at[index, pl.ds(start, count), feats]
+        return remote(src, src, sends.at[3], grecv.at[c, item], near(h, axis, s))
 
     both_hd = [(h, d) for h in range(2) for d in range(2)]
 
-    def g_start(item):
+    def g_start(c, item, piece=None):
         for h, d in both_hd:
-            g_item(h, item, d).start()
-
-    def g_wait(item):
-        arrived(grecv.at[item], xg.at[0:2] if item in (0, 1, 3, 4, 6) else xg.at[0])
-
-    pltpu.make_async_copy(xg.at[0, 0:2], xg.at[0, 0:2], loads.at[0]).wait()
-    for item in range(2):
-        for h, d in both_hd:
-            g_item(h, item, d, 0).start()
-    for h in range(2):
-        arrived(recvs.at[h], xg.at[0, 0])
-        for d in range(2):
-            g_item(h, 0, d, 1).start()
-    for h, d in both_hd:
-        g_item(h, 1, d, 1).start()
+            g_item(c, h, item, d, piece).start()
+
+    def g_wait(c, item):
+        count = CHUNK[c][0][1] * 2
+        if item in (0, 1, 3, 4, 6):
+            arrived(grecv.at[c, item], xg.at[0:2, 0:count])
+        else:
+            arrived(grecv.at[c, item], xg.at[0, 0:count])
+
+    pltpu.make_async_copy(xg.at[0, 0:4], xg.at[0, 0:4], loads.at[0]).wait()
+    g_start(0, 0, 0)
+    g_start(0, 1, 0)
+    arrived(recvs.at[0], xg.at[0, 0:3])
+    g_start(0, 0, 1)
+    g_start(0, 1, 1)
+    arrived(recvs.at[1], xg.at[0, 0])
     load_fi.start()
     load_fo.start()
 
@@ -185,25 +194,43 @@
         cols = slice(k * LANES, (k + 1) * LANES)
         w2[k] = (wraw[:, cols].astype(F32) * gain_a[cols].astype(F32).reshape(1, LANES)).astype(BF16)
 
-    g_wait(0)
-    g_start(2)
-    g_start(3)
-    g_start(4)
+    g_wait(0, 0)
+    g_start(0, 2)
+    g_start(0, 3)
+    g_start(0, 4)
 
     acc[...] = jnp.zeros_like(acc)
     ssq[...] = jnp.zeros_like(ssq)
 
-    def qkv_pair(i1, i2):
+    def qkv_pair(i1, i2, pairs):
         wpair = jnp.concatenate([w2[i1], w2[i2]], axis=1)
-
-        def step(q, carry):
-            xx = jnp.concatenate([xg[i1, q], xg[i2, q]], axis=0)
-            acc[q] += dot(wpair, xx)
+        for u in pairs:
+            b1, b2 = PAIRS[u]
+            x1 = jnp.concatenate([xg[i1, b1], xg[i1, b2]], axis=1)
+            x2 = jnp.concatenate([xg[i2, b1], xg[i2, b2]], axis=1)
+            xx = jnp.concatenate([x1, x2], axis=0)
+            acc[u] += dot(wpair, xx)
             f = xx.astype(F32)
-            ssq[q] += jnp.sum((f * f).reshape(2 * LANES // 8, 8, QUART), axis=0)
-            return carry
-
-        lax.fori_loop(0, 4, step, 0)
+            ssq[u] += jnp.sum((f * f).reshape(2 * LANES // 8, 8, QUART), axis=0)
+
+    def group0(pairs):
+        qkv_pair(chip_at(x - 1, y), chip_at(x + 1, y), pairs)
+        qkv_pair(chip_at(x, y - 1), chip_at(x, y + 1), pairs)
+
+    def group1(pairs):
+        qkv_pair(chip_at(x - 1, y - 1), chip_at(x + 1, y - 1), pairs)
+        qkv_pair(chip_at(x - 1, y + 1), chip_at(x + 1, y + 1), pairs)
+        qkv_pair(chip_at(x + 2, y), chip_at(x, y + 2), pairs)
+
+    def group2(pairs):
+        qkv_pair(chip_at(x + 2, y - 1), chip_at(x + 2, y + 1), pairs)
+        qkv_pair(chip_at(x - 1, y + 2), chip_at(x + 1, y + 2), pairs)
+
+    def group3(pairs):
+        qkv_pair(chip, chip_at(x + 2, y + 2), pairs)
+
+    EARLY = (0, 1, 2)
+    LATE = (3,)
 
     row = route[...].astype(F32)
     r_i = lax.broadcasted_iota(jnp.int32, (CAP, CAP), 0)
@@ -223,16 +250,18 @@
         at = slice(k * LANES, (k + 1) * LANES)
         wot[at] = wo[:, at].astype(F32).T.astype(BF16)
 
-    g_wait(1)
-    g_start(5)
-    qkv_pair(chip_at(x - 1, y), chip_at(x + 1, y))
-    g_wait(2)
-    g_start(6)
-    qkv_pair(chip_at(x, y - 1), chip_at(x, y + 1))
-    g_wait(3)
-    g_start(7)
-    g_wait(4)
-    g_start(8)
+    g_wait(0, 1)
+    g_start(0, 5)
+    g_start(1, 0)
+    g_start(1, 1)
+    qkv_pair(chip_at(x - 1, y), chip_at(x + 1, y), EARLY)
+    g_wait(0, 2)
+    g_start(0, 6)
+    qkv_pair(chip_at(x, y - 1), chip_at(x, y + 1), EARLY)
+    g_wait(0, 3)
+    g_start(0, 7)
+    g_wait(0, 4)
+    g_start(0, 8)
 
     mine_r = pl.ds(pl.multiple_of(core * CAPC, 16), CAPC)
     theirs_r = pl.ds(pl.multiple_of((1 - core) * CAPC, 16), CAPC)
@@ -243,45 +272,58 @@
             total = total + dot_nt(oh[:, q * QUART : (q + 1) * QUART], block_of(q))
         return total.astype(BF16)
 
-    pk[0] = pick(lambda q: xg[chip, q])
+    pk[0] = pick(lambda q: jnp.concatenate([xg[chip, 2 * q], xg[chip, 2 * q + 1]], axis=1))
     swap_r = [
         remote(pk.at[i, theirs_r], px.at[i], sends.at[4], recvs.at[4 + i], partner) for i in range(2)
     ]
     swap_r[0].start()
 
-    g_wait(5)
-    qkv_pair(chip_at(x - 1, y - 1), chip_at(x + 1, y - 1))
-    qkv_pair(chip_at(x - 1, y + 1), chip_at(x + 1, y + 1))
-    g_wait(6)
-    g_start(9)
-    qkv_pair(chip_at(x + 2, y), chip_at(x, y + 2))
-    g_wait(7)
-    g_wait(8)
-    qkv_pair(chip_at(x + 2, y - 1), chip_at(x + 2, y + 1))
-    qkv_pair(chip_at(x - 1, y + 2), chip_at(x + 1, y + 2))
-    g_wait(9)
-    qkv_pair(chip, chip_at(x + 2, y + 2))
-
-    def finish_qkv(q):
-        scale = lax.rsqrt(jnp.sum(ssq[q], axis=0, keepdims=True) * (1.0 / FEAT) + EPS)
-        qt[:, q * QUART : (q + 1) * QUART] = (
-            (acc[q, 0:LANES] * scale).astype(BF16).astype(F32) * (1.0 / HEADW**0.5)
-        ).astype(BF16)
-        keys = (acc[q, LANES : 2 * LANES] * scale).T.astype(BF16)
-        vals = (acc[q, 2 * LANES :] * scale).astype(BF16)
+    g_wait(0, 5)
+    g_wait(1, 0)
+    g_start(1, 2)
+    g_start(1, 3)
+    g_start(1, 4)
+    group1(EARLY)
+    g_wait(0, 6)
+    g_start(0, 9)
+    g_wait(1, 1)
+    g_start(1, 5)
+    group0(LATE)
+    g_wait(0, 7)
+    g_wait(0, 8)
+    g_wait(1, 2)
+    g_start(1, 6)
+    g_wait(1, 3)
+    g_start(1, 7)
+    g_wait(1, 4)
+    g_start(1, 8)
+    group2(EARLY)
+    g_wait(0, 9)
+    group3(EARLY)
+
+    def finish_qkv(u):
+        scale = lax.rsqrt(jnp.sum(ssq[u], axis=0, keepdims=True) * (1.0 / FEAT) + EPS)
+        query = (acc[u, 0:LANES] * scale).astype(BF16).astype(F32) * (1.0 / HEADW**0.5)
+        keys = (acc[u, LANES : 2 * LANES] * scale).T.astype(BF16)
+        vals = (acc[u, 2 * LANES :] * scale).astype(BF16)
         for half in range(2):
+            b = PAIRS[u][half]
             at = slice(half * QBLK, (half + 1) * QBLK)
-            kvb[1 + 2 * q + half, 0] = keys[at]
-            kvb[1 + 2 * q + half, 1] = vals[:, at]
+            qt[:, b * QBLK : (b + 1) * QBLK] = query[:, at].astype(BF16)
+            kvb[1 + b, 0] = keys[at]
+            kvb[1 + b, 1] = vals[:, at]
 
     h_prev = remote(kvb.at[1], kvb.at[NBLK + 1], sends.at[5], recvs.at[6], prev_dev)
     h_next = remote(kvb.at[NBLK], kvb.at[0], sends.at[5], recvs.at[7], next_dev)
     finish_qkv(0)
-    finish_qkv(3)
+    finish_qkv(1)
     h_prev.start()
     h_next.start()
-    finish_qkv(1)
+    g_wait(1, 5)
+    g_wait(1, 6)
+    g_start(1, 9)
     finish_qkv(2)
+    group1(LATE)
 
     def attend(i, kind):
         at = pl.ds(pl.multiple_of(i * QBLK, QBLK), QBLK)
@@ -299,11 +341,11 @@
         o = dot(vals, e.astype(BF16)) / total
         ctx[:, at] = jnp.concatenate([o[:HEADW, :QBLK], o[HEADW:, QBLK:]], axis=0).astype(BF16)
 
-    def attend_mid(i, carry):
-        attend(i, 1)
-        return carry
-
-    lax.fori_loop(1, NBLK - 1, attend_mid, 0)
+    attend(1, 1)
+    attend(NBLK - 2, 1)
+    g_wait(1, 7)
+    g_wait(1, 8)
+    group2(LATE)
     arrived(recvs.at[6], kvb.at[0])
     arrived(recvs.at[7], kvb.at[0])
     attend(0, 0)
@@ -312,72 +354,78 @@
     def wot_rows(index):
         return wot[pl.ds(pl.multiple_of(index * LANES, LANES), LANES), :]
 
-    def project(step):
+    def project(e, step):
         for h in range(2):
-            rhs = ctx[:, 2 * h * QUART : 2 * (h + 1) * QUART]
+            q = SETS[e][h]
+            rhs = ctx[:, q * QUART : (q + 1) * QUART]
             for pair in ((2, -1), (1, 0)):
                 i1 = block(h, pair[0], step)
                 i2 = block(h, pair[1], step)
                 o = dot(jnp.concatenate([wot_rows(i1), wot_rows(i2)], axis=0), rhs).astype(BF16)
-                for part in range(2):
-                    at = slice(part * QUART, (part + 1) * QUART)
-                    pb[i1, 2 * h + part] = o[:LANES, at]
-                    pb[i2, 2 * h + part] = o[LANES:, at]
-
-    def r1_copy(h, j, kind, d):
+                pb[i1, q] = o[:LANES]
+                pb[i2, q] = o[LANES:]
+
+    def feats_of(part):
+        return slice(part * HEADW, (part + 1) * HEADW)
+
+    def r1_copy(e, h, j, kind, d):
         s = SIGN[d]
         db, part = ((2, d), (s, d), (s, 1 - d))[kind]
-        src = pb.at[block(h, OFF[j], db), 2 * h + part]
-        return remote(src, rx1.at[h, j, kind, d], sends.at[6], rrecv.at[j if kind == 0 else 4 + j], near(h, 1, s))
-
-    def r2_copy(h, kind, d):
+        src = pb.at[block(h, OFF[j], db), SETS[e][h], feats_of(part)]
+        sem = rrecv.at[e, j if kind == 0 else 4 + j]
+        return remote(src, rx1.at[e, h, j, kind, d], sends.at[6], sem, near(h, 1, s))
+
+    def r2_copy(e, h, kind, d):
         s = SIGN[d]
         da, part = ((2, d), (s, d), (s, 1 - d))[kind]
-        src = pb.at[block(h, da, 0), 2 * h + part]
-        return remote(src, rx2.at[h, kind, d], sends.at[6], rrecv.at[8 if kind == 0 else 9], near(h, 0, s))
-
-    def r1_start(j, kind):
+        src = pb.at[block(h, da, 0), SETS[e][h], feats_of(part)]
+        sem = rrecv.at[e, 8 if kind == 0 else 9]
+        return remote(src, rx2.at[e, h, kind, d], sends.at[6], sem, near(h, 0, s))
+
+    def r1_start(e, j, kind):
         for h, d in both_hd:
-            r1_copy(h, j, kind, d).start()
-
-    def r2_start(kind):
+            r1_copy(e, h, j, kind, d).start()
+
+    def r2_start(e, kind):
         for h, d in both_hd:
-            r2_copy(h, kind, d).start()
-
-    def relay1(j):
-        arrived(rrecv.at[j], xg.at[0])
+            r2_copy(e, h, kind, d).start()
+
+    def relay1(e, j):
+        arrived(rrecv.at[e, j], xg.at[0, 0:4])
         for h, d in both_hd:
             index = block(h, OFF[j], SIGN[d])
-            q = 2 * h + d
-            pb[index, q] = (pb[index, q].astype(F32) + rx1[h, j, 0, d].astype(F32)).astype(BF16)
-            r1_copy(h, j, 1, d).start()
-
-    def relay2():
-        arrived(rrecv.at[8], xg.at[0])
+            q, at = SETS[e][h], feats_of(d)
+            pb[index, q, at] = (pb[index, q, at].astype(F32) + rx1[e, h, j, 0, d].astype(F32)).astype(BF16)
+            r1_copy(e, h, j, 1, d).start()
+
+    def relay2(e):
+        arrived(rrecv.at[e, 8], xg.at[0, 0:4])
         for h, d in both_hd:
             index = block(h, SIGN[d], 0)
-            q = 2 * h + d
-            pb[index, q] = (pb[index, q].astype(F32) + rx2[h, 0, d].astype(F32)).astype(BF16)
-            r2_copy(h, 1, d).start()
-
-    def sum1(h, j, part):
-        got = pb[block(h, OFF[j], 0), 2 * h + part].astype(F32)
-        return got + rx1[h, j, 1, part].astype(F32) + rx1[h, j, 2, 1 - part].astype(F32)
-
-    def total1(j):
-        arrived(rrecv.at[4 + j], xg.at[0:2])
+            q, at = SETS[e][h], feats_of(d)
+            pb[index, q, at] = (pb[index, q, at].astype(F32) + rx2[e, h, 0, d].astype(F32)).astype(BF16)
+            r2_copy(e, h, 1, d).start()
+
+    def sum1(e, h, j, part):
+        got = pb[block(h, OFF[j], 0), SETS[e][h], feats_of(part)].astype(F32)
+        return got + rx1[e, h, j, 1, part].astype(F32) + rx1[e, h, j, 2, 1 - part].astype(F32)
+
+    def total1(e, j):
+        arrived(rrecv.at[e, 4 + j], xg.at[0])
         for h in range(2):
             for part in range(2):
-                pb[block(h, OFF[j], 0), 2 * h + part] = sum1(h, j, part).astype(BF16)
-
-    def last():
-        arrived(rrecv.at[7], xg.at[0:2])
-        arrived(rrecv.at[9], xg.at[0:2])
+                pb[block(h, OFF[j], 0), SETS[e][h], feats_of(part)] = sum1(e, h, j, part).astype(BF16)
+
+    def last(e):
+        arrived(rrecv.at[e, 7], xg.at[0])
+        arrived(rrecv.at[e, 9], xg.at[0])
         for h in range(2):
+            q = SETS[e][h]
             for part in range(2):
-                mixed = sum1(h, 3, part) + rx2[h, 1, part].astype(F32) + rx2[h, 2, 1 - part].astype(F32)
-                q = 2 * h + part
-                upd[q] = (xg[chip, q].astype(F32) + mixed).astype(BF16)
+                at = feats_of(part)
+                own = jnp.concatenate([xg[chip, 2 * q, at], xg[chip, 2 * q + 1, at]], axis=1)
+                mixed = sum1(e, h, 3, part) + rx2[e, h, 1, part].astype(F32) + rx2[e, h, 2, 1 - part].astype(F32)
+                upd[q, at] = (own.astype(F32) + mixed).astype(BF16)
 
     def s1_copy(n, t, j):
         src = sb.at[n, small_block(t, j)]
@@ -386,6 +434,10 @@
     def s2_copy(n, t):
         src = sb2.at[n, t]
         return remote(src, rxb.at[n, t - 1], sends.at[7], s2recv.at[n], small_near(0, t))
+
+    def o_copy(t):
+        dev = {"tp": small_block(0, t) * 2 + 1 - core}
+        return remote(sb2.at[1, t], rxo.at[t], sends.at[11], recvs.at[9], dev)
 
     STEPS = (2, 1, 3)
     COLS = (2, 1, 3, 0)
@@ -404,6 +456,8 @@
             sb2[n, j] = total.astype(BF16)
             if j > 0:
                 s2_copy(n, j).start()
+            if n == 1:
+                o_copy(j).start()
 
     def small_end(n):
         total = sb2[n, 0].astype(F32)
@@ -446,10 +500,26 @@
     def gather_last():
         arrived(recvs.at[8], sb.at[0])
 
+    project(0, 2)
+    r1_start(0, 0, 0)
+    r1_start(0, 1, 0)
+    r1_start(0, 2, 0)
+    project(0, 1)
+    project(0, -1)
+    r1_start(0, 0, 2)
+    g_wait(1, 9)
+    group3(LATE)
+    finish_qkv(3)
+    r1_start(0, 1, 2)
+    attend(2, 1)
+    attend(3, 1)
+    attend(4, 1)
+    attend(5, 1)
     pk[1] = pick(lambda q: ctx[:, q * QUART : (q + 1) * QUART])
     swap_r[1].start()
-    project(2)
-    r1_start(0, 0)
+    relay1(0, 0)
+    project(1, 2)
+    r1_start(0, 2, 2)
     arrived(recvs.at[4], px.at[0])
     arrived(recvs.at[5], px.at[0])
     rows_ctx = (pk[1, mine_r].astype(F32) + px[1].astype(F32)).astype(BF16)
@@ -458,26 +528,39 @@
         sb[0, 2 * k] = o[:, :LANES]
         sb[0, 2 * k + 1] = o[:, LANES:]
     small_start(0)
-    project(1)
-    project(-1)
-    r1_start(0, 2)
+    r1_start(0, 3, 0)
+    project(0, 0)
+    relay1(0, 1)
+    relay1(0, 2)
+    project(1, 1)
     small_mid(0)
-    r1_start(1, 0)
-    relay1(0)
+    total1(0, 0)
+    r2_start(0, 0)
+    r1_start(0, 3, 2)
+    r1_start(1, 0, 0)
+    project(1, -1)
     rows_new = pk[0, mine_r].astype(F32) + px[0].astype(F32) + small_end(0)
     gp[chip, mine_r] = rows_new.astype(BF16)
     gather_first()
-    r1_start(2, 0)
-    project(0)
+    relay1(0, 3)
+    total1(0, 1)
+    total1(0, 2)
+    r2_start(0, 2)
+    r1_start(1, 0, 2)
+    r1_start(1, 1, 0)
+    project(1, 0)
     gather_second()
-    r1_start(1, 2)
-    relay1(1)
+    relay1(1, 0)
+    r1_start(1, 1, 2)
+    r1_start(1, 2, 0)
+    r1_start(1, 2, 2)
     gather_third()
-    r1_start(2, 2)
-    r1_start(3, 0)
-    relay1(2)
-    total1(0)
-    r2_start(0)
+    relay2(0)
+    r1_start(1, 3, 0)
+    relay1(1, 1)
+    relay1(1, 2)
+    total1(1, 0)
+    r2_start(1, 0)
     gather_last()
 
     sq = jnp.zeros((CAP, LANES), F32)
@@ -489,7 +572,7 @@
         at = slice(k * LANES, (k + 1) * LANES)
         nrm[:, at] = (gp[k].astype(F32) * scale * gain_f[at].astype(F32).reshape(1, LANES)).astype(BF16)
 
-    r1_start(3, 2)
+    r1_start(1, 3, 2)
     load_fi.wait()
 
     def ffn_in(n0, nw):
@@ -499,13 +582,14 @@
         hid[:, n0 : n0 + nw] = (gelu(gate) * up).astype(BF16)
 
     ffn_in(0, 256)
-    total1(1)
-    total1(2)
-    r2_start(2)
+    total1(1, 1)
+    total1(1, 2)
+    r2_start(1, 2)
     ffn_in(256, 256)
-    relay1(3)
+    relay1(1, 3)
     ffn_in(512, 128)
-    relay2()
+    relay2(1)
+    last(0)
     load_fo.wait()
 
     def c_copy(n):
@@ -522,17 +606,19 @@
         for k in range(4 * n, 4 * n + 4):
             sb[1, k] = (pb2[k, mine_r].astype(F32) + rxc[k].astype(F32)).astype(BF16)
     small_start(1)
-    last()
+    last(1)
     small_mid(1)
     heavy = small_end(1)
-    slot = lax.broadcasted_iota(jnp.int32, (CAPC, LANES), 0) + core * CAPC
-    heavy = jnp.where(slot < counts[z], heavy, 0.0)
-    high = heavy.astype(BF16)
-    hv[mine_r, 0:LANES] = high
-    hv[mine_r, LANES:] = (heavy - high.astype(F32)).astype(BF16)
-    swap_h = remote(hv.at[mine_r], hv.at[mine_r], sends.at[11], recvs.at[9], partner)
-    swap_h.start()
-    arrived(recvs.at[9], hv.at[0:CAPC])
+    arrived(recvs.at[9], sb.at[0, 0:4])
+    heavy_oth = rxo[0].astype(F32)
+    for t in STEPS:
+        heavy_oth = heavy_oth + rxo[t].astype(F32)
+    for rows, base_slot, value in ((mine_r, core * CAPC, heavy), (theirs_r, (1 - core) * CAPC, heavy_oth)):
+        slot = lax.broadcasted_iota(jnp.int32, (CAPC, LANES), 0) + base_slot
+        value = jnp.where(slot < counts[z], value, 0.0)
+        high = value.astype(BF16)
+        hv[rows, 0:LANES] = high
+        hv[rows, LANES:] = (value - high.astype(F32)).astype(BF16)
 
     for q in range(4):
         at = slice(q * QUART, (q + 1) * QUART)
@@ -544,7 +630,7 @@
     save_out = pltpu.make_async_copy(fin.at[own_feat], out_part, loads.at[5])
     save_out.start()
 
-    left(0, xg.at[0, 0:2])
+    left(0, xg.at[0, 0:4])
     left(1, wraw.at[0 : 3 * HEADW])
     left(2, wo.at[0:HEADW])
     left(3, xg.at[0:15])
@@ -555,7 +641,7 @@
     left(8, sb.at[0, 0:15])
     left(9, sb.at[0])
     left(10, sb.at[1])
-    left(11, hv.at[0:CAPC])
+    left(11, sb.at[0, 0:4])
     save_out.wait()
     send_out.wait()
 
@@ -580,7 +666,7 @@
             vm((2, FEAT, FFU), BF16),
             vm((FFU, FEAT), BF16),
             vm((CHIPS, 3 * LANES, LANES), BF16),
-            vm((CHIPS, 4, LANES, QUART), BF16),
+            vm((CHIPS, NBLK, LANES, QBLK), BF16),
             vm((4, 3 * LANES, QUART), F32),
             vm((4, 8, QUART), F32),
             vm((LANES, HALF), BF16),
@@ -589,8 +675,8 @@
             vm((3, 3 * QBLK, QBLK), F32),
             vm((CAP, HALF), BF16),
             vm((CHIPS, 4, LANES, QUART), BF16),
-            vm((2, 4, 3, 2, LANES, QUART), BF16),
-            vm((2, 3, 2, LANES, QUART), BF16),
+            vm((2, 2, 4, 3, 2, HEADW, QUART), BF16),
+            vm((2, 2, 3, 2, HEADW, QUART), BF16),
             vm((4, LANES, QUART), BF16),
             vm((LANES, HALF), BF16),
             vm((CHIPS, CAP, LANES), BF16),
@@ -604,12 +690,13 @@
             vm((2, 3, SIDE, CAPC, LANES), BF16),
             vm((2, SIDE, CAPC, LANES), BF16),
             vm((2, 3, CAPC, LANES), BF16),
+            vm((SIDE, CAPC, LANES), BF16),
             vm((CAP, 2 * LANES), BF16),
             dma((6,)),
             dma((13,)),
             dma((11,)),
-            dma((10,)),
-            dma((10,)),
+            dma((2, 10)),
+            dma((2, 10)),
             dma((2, SIDE)),
             dma((2,)),
             dma((7,)),

time: 81.6 us -> 80 us (0.980)
  Pallas kernels: 79.8 us -> 78.2 us
    pallas_call x1, Pallas kernels: 79.8 us -> 78.2 us  [local(): pl.pallas_call(kernel, out_shape=jax.ShapeDtypeStruct((HEADW, TOK), BF16)...]
where the time goes in v4:
time: 80 us; the launch traced here: 79.8 us
  Pallas kernels  78.2 us (98%)
  local copies, waits for them, and re-layouts  1.67 us (2%)
    pallas_call x1, Pallas kernels, local(): pl.pallas_call(kernel, out_shape=jax.ShapeDtypeStruct((HEADW, TOK), BF16)...  78.2 us
    unnamed x1, local copies, waits for them, and re-layouts  1.67 us

profile of v4, /device:TPU:1, one launch (start us, length us, event | category | flops | bytes accessed | tf_op | source)
XLA Modules:
  0.0 79.8 jit_solution(10545136709355813016)
XLA Ops:
  0.0 78.2 %layer.1 = bf16[64,2048]{1,0:T(8,128)(2,1)} custom-call(bf16[64,2048]{1,0:T(8,128)(2,1)} %bitcast.5, bf16[3,64,2048]{2,1,0:T(8,128)(2,1)} %bitcast.4, bf16[64,2048]{1,0:T(8,128)(2,1)} %wout.1, bf16[2,2048,640]{2,1,0:T(8,128)(2,1)} %ffi.1, bf16[640,2048]{1,0:T(8,128)(2,1)} %ffo.1, bf16[2048]{0:T(1024)(128)(2,1)} %gain_a.1, bf16[2048]{0:T(1024)(128)(2,1)} %gain_f.1, ...), custom_call_target="tpu_custom_call" | custom-call | tf_op jit(solution)/shard_map/layer/pallas_call | solution.py:655
  78.2 1.7 %copy.11 = bf16[2048,64]{0,1:T(8,128)(2,1)} copy(bf16[2048,64]{0,1:T(8,128)(2,1)} %bitcast.3) | data formatting | bytes 524288

commit v5 on v4

--- a/solution.py
+++ b/solution.py
@@ -48,9 +48,9 @@
 
 
 def kernel(
-    res, wqkv, wout, ffi, ffo, gain_a, gain_f, route, counts,
+    res, wqkv, wout, ffi, ffo, gain_a_in, gain_f_in, route_in, counts,
     out,
-    wraw, wo, wot, fi, fo, w2, xg, acc, ssq, qt, kvb, ctx, bias, oh,
+    gain_a, gain_f, route, updx, wraw, wo, wot, fi, fo, w2, xg, acc, ssq, qt, kvb, ctx, bias, oh,
     pb, rx1, rx2, upd, fin, gp, pk, px, nrm, hid, pb2, rxc, sb, rxa, sb2, rxb, rxo, hv,
     loads, sends, recvs, grecv, rrecv, s1recv, s2recv, arecv, crecv,
 ):
@@ -118,6 +118,12 @@
     for copy in load_x + load_w:
         copy.start()
     load_o.start()
+    load_small = [
+        pltpu.make_async_copy(src, dst, loads.at[6 + i])
+        for i, (src, dst) in enumerate(((gain_a_in, gain_a), (gain_f_in, gain_f), (route_in, route)))
+    ]
+    for copy in load_small:
+        copy.start()
 
     other = tp + 1 - 2 * core
     prev_dev = {"seq": lax.rem(z + 3 + core, 4), "tp": other}
@@ -188,6 +194,9 @@
     load_fi.start()
     load_fo.start()
 
+    for copy in load_small:
+        copy.wait()
+
     pltpu.make_async_copy(wraw.at[0 : 3 * HEADW], wraw.at[0 : 3 * HEADW], loads.at[1]).wait()
     arrived(recvs.at[2], wraw.at[0 : 3 * HEADW])
     for k in range(CHIPS):
@@ -235,8 +244,8 @@
     row = route[...].astype(F32)
     r_i = lax.broadcasted_iota(jnp.int32, (CAP, CAP), 0)
     c_i = lax.broadcasted_iota(jnp.int32, (CAP, CAP), 1)
-    col = jnp.sum(jnp.where(r_i == c_i, row, 0.0), axis=1, keepdims=True) - (core * HALF).astype(F32)
-    lane = lax.broadcasted_iota(jnp.int32, (CAP, HALF), 1).astype(F32)
+    col = jnp.sum(jnp.where(r_i == c_i, row, 0.0), axis=1, keepdims=True)
+    lane = lax.broadcasted_iota(jnp.int32, (CAP, TOK), 1).astype(F32)
     oh[...] = jnp.where(lane == col, 1.0, 0.0).astype(BF16)
     k_i = lax.broadcasted_iota(jnp.int32, (3 * QBLK, QBLK), 0) - QBLK
     q_i = lax.broadcasted_iota(jnp.int32, (3 * QBLK, QBLK), 1)
@@ -266,10 +275,13 @@
     mine_r = pl.ds(pl.multiple_of(core * CAPC, 16), CAPC)
     theirs_r = pl.ds(pl.multiple_of((1 - core) * CAPC, 16), CAPC)
 
+    def quart_of(half, q):
+        return pl.ds(pl.multiple_of(half * HALF + q * QUART, QUART), QUART)
+
     def pick(block_of):
         total = jnp.zeros((CAP, LANES), F32)
         for q in range(4):
-            total = total + dot_nt(oh[:, q * QUART : (q + 1) * QUART], block_of(q))
+            total = total + dot_nt(oh[:, quart_of(core, q)], block_of(q))
         return total.astype(BF16)
 
     pk[0] = pick(lambda q: jnp.concatenate([xg[chip, 2 * q], xg[chip, 2 * q + 1]], axis=1))
@@ -607,6 +619,8 @@
             sb[1, k] = (pb2[k, mine_r].astype(F32) + rxc[k].astype(F32)).astype(BF16)
     small_start(1)
     last(1)
+    swap_u = remote(upd.at[:, oth_feat], updx, sends.at[12], recvs.at[10], partner)
+    swap_u.start()
     small_mid(1)
     heavy = small_end(1)
     arrived(recvs.at[9], sb.at[0, 0:4])
@@ -617,17 +631,22 @@
         slot = lax.broadcasted_iota(jnp.int32, (CAPC, LANES), 0) + base_slot
         value = jnp.where(slot < counts[z], value, 0.0)
         high = value.astype(BF16)
-        hv[rows, 0:LANES] = high
-        hv[rows, LANES:] = (value - high.astype(F32)).astype(BF16)
-
+        low = (value - high.astype(F32)).astype(BF16)
+        hv[rows, :] = jnp.concatenate(
+            [
+                jnp.where(first, high[:, :HEADW], high[:, HEADW:]),
+                jnp.where(first, low[:, :HEADW], low[:, HEADW:]),
+            ],
+            axis=1,
+        )
+
+    arrived(recvs.at[10], updx)
     for q in range(4):
-        at = slice(q * QUART, (q + 1) * QUART)
-        added = dot_tn(hv[...], oh[:, at])
-        fin[:, at] = (upd[q].astype(F32) + added[:LANES] + added[LANES:]).astype(BF16)
-    out_part = out.at[:, pl.ds(pl.multiple_of(core * HALF, HALF), HALF)]
-    send_out = remote(fin.at[oth_feat], out_part, sends.at[12], recvs.at[10], partner)
-    send_out.start()
-    save_out = pltpu.make_async_copy(fin.at[own_feat], out_part, loads.at[5])
+        for half, rows_now in ((core, upd[q, own_feat]), (1 - core, updx[q])):
+            at = quart_of(half, q)
+            added = dot_tn(hv[...], oh[:, at])
+            fin[:, at] = (rows_now.astype(F32) + added[:HEADW] + added[HEADW:]).astype(BF16)
+    save_out = pltpu.make_async_copy(fin, out, loads.at[5])
     save_out.start()
 
     left(0, xg.at[0, 0:4])
@@ -642,8 +661,8 @@
     left(9, sb.at[0])
     left(10, sb.at[1])
     left(11, sb.at[0, 0:4])
+    left(12, updx)
     save_out.wait()
-    send_out.wait()
 
 
 def local(
@@ -655,11 +674,14 @@
     turned = pl.pallas_call(
         kernel,
         out_shape=jax.ShapeDtypeStruct((HEADW, TOK), BF16),
-        in_specs=[any_spec] * 5
-        + [pl.BlockSpec(memory_space=pltpu.VMEM)] * 3
+        in_specs=[any_spec] * 8
         + [pl.BlockSpec(memory_space=pltpu.SMEM)],
         out_specs=any_spec,
         scratch_shapes=[
+            vm((FEAT,), BF16),
+            vm((FEAT,), BF16),
+            vm((1, CAP), jnp.int32),
+            vm((4, HEADW, QUART), BF16),
             vm((3 * LANES, FEAT), BF16),
             vm((LANES, FEAT), BF16),
             vm((FEAT, LANES), BF16),
@@ -673,12 +695,12 @@
             vm((NBLK + 2, 2, QBLK, QBLK), BF16),
             vm((LANES, HALF), BF16),
             vm((3, 3 * QBLK, QBLK), F32),
-            vm((CAP, HALF), BF16),
+            vm((CAP, TOK), BF16),
             vm((CHIPS, 4, LANES, QUART), BF16),
             vm((2, 2, 4, 3, 2, HEADW, QUART), BF16),
             vm((2, 2, 3, 2, HEADW, QUART), BF16),
             vm((4, LANES, QUART), BF16),
-            vm((LANES, HALF), BF16),
+            vm((HEADW, TOK), BF16),
             vm((CHIPS, CAP, LANES), BF16),
             vm((2, CAP, LANES), BF16),
             vm((2, CAPC, LANES), BF16),
@@ -691,8 +713,8 @@
             vm((2, SIDE, CAPC, LANES), BF16),
             vm((2, 3, CAPC, LANES), BF16),
             vm((SIDE, CAPC, LANES), BF16),
-            vm((CAP, 2 * LANES), BF16),
-            dma((6,)),
+            vm((CAP, LANES), BF16),
+            dma((9,)),
             dma((13,)),
             dma((11,)),
             dma((2, 10)),

time: 80 us -> 79.4 us (level)
  no operation moved by 1% of the time
where the time goes in v5:
time: 79.4 us; the launch traced here: 79.2 us
  Pallas kernels  77.6 us (98%)
  local copies, waits for them, and re-layouts  1.67 us (2%)
    pallas_call x1, Pallas kernels, local(): pl.pallas_call(kernel, out_shape=jax.ShapeDtypeStruct((HEADW, TOK), BF16)...  77.6 us
    unnamed x1, local copies, waits for them, and re-layouts  1.67 us

profile of v5, /device:TPU:1, one launch (start us, length us, event | category | flops | bytes accessed | tf_op | source)
XLA Modules:
  0.0 79.2 jit_solution(1267209595366318645)
XLA Ops:
  0.0 77.6 %layer.1 = bf16[64,2048]{1,0:T(8,128)(2,1)} custom-call(bf16[64,2048]{1,0:T(8,128)(2,1)} %bitcast.5, bf16[3,64,2048]{2,1,0:T(8,128)(2,1)} %bitcast.4, bf16[64,2048]{1,0:T(8,128)(2,1)} %wout.1, bf16[2,2048,640]{2,1,0:T(8,128)(2,1)} %ffi.1, bf16[640,2048]{1,0:T(8,128)(2,1)} %ffo.1, bf16[2048]{0:T(1024)(128)(2,1)} %gain_a_in.1, bf16[2048]{0:T(1024)(128)(2,1)} %gain_f_in.1, ...), custom_call_target="tpu_custom_call" | custom-call | tf_op jit(solution)/shard_map/layer/pallas_call | solution.py:674
  77.6 1.7 %copy.11 = bf16[2048,64]{0,1:T(8,128)(2,1)} copy(bf16[2048,64]{0,1:T(8,128)(2,1)} %bitcast.3) | data formatting | bytes 524288

commit v6 on v5

--- a/solution.py
+++ b/solution.py
@@ -207,6 +207,8 @@
     g_start(0, 2)
     g_start(0, 3)
     g_start(0, 4)
+    g_start(1, 0)
+    g_start(1, 1)
 
     acc[...] = jnp.zeros_like(acc)
     ssq[...] = jnp.zeros_like(ssq)
@@ -261,8 +263,6 @@
 
     g_wait(0, 1)
     g_start(0, 5)
-    g_start(1, 0)
-    g_start(1, 1)
     qkv_pair(chip_at(x - 1, y), chip_at(x + 1, y), EARLY)
     g_wait(0, 2)
     g_start(0, 6)
@@ -271,6 +271,10 @@
     g_start(0, 7)
     g_wait(0, 4)
     g_start(0, 8)
+    g_wait(1, 0)
+    g_start(1, 2)
+    g_start(1, 3)
+    g_start(1, 4)
 
     mine_r = pl.ds(pl.multiple_of(core * CAPC, 16), CAPC)
     theirs_r = pl.ds(pl.multiple_of((1 - core) * CAPC, 16), CAPC)
@@ -291,10 +295,6 @@
     swap_r[0].start()
 
     g_wait(0, 5)
-    g_wait(1, 0)
-    g_start(1, 2)
-    g_start(1, 3)
-    g_start(1, 4)
     group1(EARLY)
     g_wait(0, 6)
     g_start(0, 9)
@@ -618,10 +618,10 @@
         for k in range(4 * n, 4 * n + 4):
             sb[1, k] = (pb2[k, mine_r].astype(F32) + rxc[k].astype(F32)).astype(BF16)
     small_start(1)
+    small_mid(1)
     last(1)
     swap_u = remote(upd.at[:, oth_feat], updx, sends.at[12], recvs.at[10], partner)
     swap_u.start()
-    small_mid(1)
     heavy = small_end(1)
     arrived(recvs.at[9], sb.at[0, 0:4])
     heavy_oth = rxo[0].astype(F32)

time: 79.4 us -> 79.4 us (level)
  no operation moved by 1% of the time
where the time goes in v6:
time: 79.4 us; the launch traced here: 79.2 us
  Pallas kernels  77.6 us (98%)
  local copies, waits for them, and re-layouts  1.67 us (2%)
    pallas_call x1, Pallas kernels, local(): pl.pallas_call(kernel, out_shape=jax.ShapeDtypeStruct((HEADW, TOK), BF16)...  77.6 us
    unnamed x1, local copies, waits for them, and re-layouts  1.67 us

profile of v6, /device:TPU:1, one launch (start us, length us, event | category | flops | bytes accessed | tf_op | source)
XLA Modules:
  0.0 79.2 jit_solution(1131377637139459009)
XLA Ops:
  0.0 77.6 %layer.1 = bf16[64,2048]{1,0:T(8,128)(2,1)} custom-call(bf16[64,2048]{1,0:T(8,128)(2,1)} %bitcast.5, bf16[3,64,2048]{2,1,0:T(8,128)(2,1)} %bitcast.4, bf16[64,2048]{1,0:T(8,128)(2,1)} %wout.1, bf16[2,2048,640]{2,1,0:T(8,128)(2,1)} %ffi.1, bf16[640,2048]{1,0:T(8,128)(2,1)} %ffo.1, bf16[2048]{0:T(1024)(128)(2,1)} %gain_a_in.1, bf16[2048]{0:T(1024)(128)(2,1)} %gain_f_in.1, ...), custom_call_target="tpu_custom_call" | custom-call | tf_op jit(solution)/shard_map/layer/pallas_call | solution.py:674
  77.6 1.7 %copy.11 = bf16[2048,64]{0,1:T(8,128)(2,1)} copy(bf16[2048,64]{0,1:T(8,128)(2,1)} %bitcast.3) | data formatting | bytes 524288
